TPU v7x, 512 devices: a whole 4x4x16 slice. The times are simulated.
512 devices in a mesh: req: 64 (over y_hi, z, core), tp: 8 (over y_lo, x).
Axes of the slice: x: 4, y: 4 (y_hi: 2, y_lo: 2; y = y_hi * 2 + y_lo), z: 16, core: 2. Of those that a mesh axis runs over, the one named last changes fastest.
Arguments:
- queries: bfloat16 [16384, 5120], P('req', 'tp')
- new_keys: bfloat16 [16384, 5120], P('req', 'tp')
- new_values: bfloat16 [16384, 5120], P('req', 'tp'), may hold values from -6 to 6
- query_gain: float32 [5120], P('tp'), may hold values from 0.1 to 1.9
- key_gain: float32 [5120], P('tp'), may hold values from 0.4 to 2.5
- cache_keys: bfloat16 [7168, 8, 5120], P('req', None, 'tp')
- cache_values: bfloat16 [7168, 8, 5120], P('req', None, 'tp'), may hold values from -6 to 6
- page_table: int32 [64, 48], P('req'), may hold values from 0 to 111, as said below
- cache_lens: int32 [64], P('req'), may hold values from 48 to 384, as said below
- mig_pages: int32 [64, 64], P('req'), may hold values from 0 to 111, as said below
- mig_dest: int32 [4096, 1], P('req'), may hold values from 0 to 63; in each aligned block of 64 rows (0 to 63, 64 to 127, ...) at most 2 rows name the same one
- cross_queries: bfloat16 [16384, 5120], P('req', 'tp')
- text_keys: bfloat16 [8192, 5120], P('req', 'tp')
- text_values: bfloat16 [8192, 5120], P('req', 'tp'), may hold values from -6 to 6
- out_weight: bfloat16 [5120, 5120], P('tp', 'req'), may hold values from -1 to 1
- residual: bfloat16 [16384, 5120], P('req', 'tp')
- gate: bfloat16 [64, 5120], P('req', 'tp'), may hold values from -6 to 6
- shift: bfloat16 [64, 5120], P('req', 'tp'), may hold values from -3 to 3
- scale: bfloat16 [64, 5120], P('req', 'tp'), may hold values from -3 to 3
Outputs:
- stream: bfloat16 [16384, 5120], P('req', 'tp')
- normed: bfloat16 [16384, 5120], P('req', 'tp')
- cross_out: bfloat16 [16384, 5120], P('req', 'tp')
Inputs may be any that keep to these rules, and one draw needn't show every extreme that they name: Row r of page_table and row r of mig_pages together name every one of the 112 pages of row r's pool exactly once. `mig_pages`: see page_table. `cache_lens`: at least 48; the largest is exactly 384. `mig_dest`: among the 64 pages of one request row (the rows of one device) no destination is named more than 2 times.
All inputs are finite; a program needn't handle non-finite values.
Results may differ from a plain program's by a relative error of at most 0.014.
Values may be sent and summed in bfloat16 or wider, within the bound.
A program may use at most 64 MiB of HBM per device.

v0:
```python
import math

import jax
import jax.numpy as jnp
from jax import lax
from jax.sharding import PartitionSpec as P

HD = 128
CAP = 2


EPS = 1e-06


def attend(query_rows, key_rows, value_rows, usable, head_count):
    row_count = query_rows.shape[0]
    head_width = query_rows.shape[1] // head_count
    query_heads = query_rows.reshape(row_count, head_count, head_width)
    key_heads = key_rows.reshape(key_rows.shape[0], head_count, head_width)
    value_heads = value_rows.reshape(value_rows.shape[0], head_count, head_width)
    scores = jnp.einsum(
        "qhd,khd->hqk", query_heads, key_heads, preferred_element_type=jnp.float32
    ) * (1.0 / math.sqrt(head_width))
    if usable is not None:
        scores = jnp.where(usable[None, None, :], scores, -jnp.inf)
    row_max = jnp.max(scores, axis=2, keepdims=True)
    exponent = jnp.exp(scores - row_max)
    denominator = jnp.sum(exponent, axis=2)
    weights = exponent.astype(jnp.bfloat16)
    mixed = jnp.einsum("hqk,khd->qhd", weights, value_heads, preferred_element_type=jnp.float32)
    mixed = mixed / jnp.transpose(denominator)[:, :, None]
    return mixed.reshape(row_count, head_count * head_width).astype(jnp.bfloat16)


def shards(
    queries,
    new_keys,
    new_values,
    query_gain,
    key_gain,
    cache_keys,
    cache_values,
    page_table,
    cache_lens,
    mig_pages,
    mig_dest,
    cross_queries,
    text_keys,
    text_values,
    out_weight,
    residual,
    gate,
    shift,
    scale,
):
    token_count, local_width = queries.shape
    head_count = local_width // HD
    full_width = local_width * lax.axis_size("tp")
    query_float = queries.astype(jnp.float32)
    key_float = new_keys.astype(jnp.float32)
    query_squares, key_squares = lax.psum(
        (jnp.sum(query_float * query_float, axis=1), jnp.sum(key_float * key_float, axis=1)), "tp"
    )
    query_normed = (
        query_float * lax.rsqrt(query_squares / full_width + EPS)[:, None] * query_gain
    ).astype(jnp.bfloat16)
    key_normed = (key_float * lax.rsqrt(key_squares / full_width + EPS)[:, None] * key_gain).astype(
        jnp.bfloat16
    )
    peer_count = lax.axis_size("req")
    page_len = cache_keys.shape[1]
    destination = mig_dest[:, 0]
    slot_match = (destination[:, None] == jnp.arange(peer_count, dtype=jnp.int32)[None, :]).astype(
        jnp.int32
    )
    position = jnp.sum(jnp.cumsum(slot_match, axis=0) * slot_match, axis=1) - 1
    target_slot = destination * CAP + position
    selection = (
        jnp.arange(peer_count * CAP, dtype=jnp.int32)[:, None] == target_slot[None, :]
    ).astype(jnp.bfloat16)
    moving = mig_pages[0]
    moving_keys = cache_keys[moving].reshape(moving.shape[0], -1)
    moving_values = cache_values[moving].reshape(moving.shape[0], -1)
    sent_keys = (
        jnp.dot(selection, moving_keys, preferred_element_type=jnp.float32)
        .astype(jnp.bfloat16)
        .reshape(peer_count * CAP, page_len, local_width)
    )
    sent_values = (
        jnp.dot(selection, moving_values, preferred_element_type=jnp.float32)
        .astype(jnp.bfloat16)
        .reshape(peer_count * CAP, page_len, local_width)
    )
    slot_filled = jnp.sum(selection.astype(jnp.float32), axis=1)
    sent_flags = jnp.broadcast_to(slot_filled[:, None], (peer_count * CAP, page_len)).astype(
        jnp.bfloat16
    )
    arrived_keys, arrived_values, arrived_flags = (
        lax.all_to_all(sent_keys, "req", split_axis=0, concat_axis=0, tiled=True),
        lax.all_to_all(sent_values, "req", split_axis=0, concat_axis=0, tiled=True),
        lax.all_to_all(sent_flags, "req", split_axis=0, concat_axis=0, tiled=True),
    )
    own_pages = page_table[0]
    resident_keys = cache_keys[own_pages].reshape(-1, local_width)
    resident_values = cache_values[own_pages].reshape(-1, local_width)
    resident_usable = jnp.arange(resident_keys.shape[0], dtype=jnp.int32) < cache_lens[0]
    all_keys = jnp.concatenate(
        [resident_keys, arrived_keys.reshape(-1, local_width), key_normed], axis=0
    )
    all_values = jnp.concatenate(
        [resident_values, arrived_values.reshape(-1, local_width), new_values], axis=0
    )
    usable = jnp.concatenate(
        [resident_usable, arrived_flags.reshape(-1) > 0, jnp.ones((token_count,), bool)]
    )
    attended = attend(query_normed, all_keys, all_values, usable, head_count)
    cross_out = attend(cross_queries, text_keys, text_values, None, head_count)
    partial_rows = jnp.dot(
        attended,
        lax.all_gather(out_weight, "req", axis=1, tiled=True),
        preferred_element_type=jnp.float32,
    )
    projected = lax.psum(partial_rows.astype(jnp.bfloat16), "tp").astype(jnp.float32)
    stream_all, gate_all = (
        lax.all_gather(residual, "tp", axis=1, tiled=True),
        lax.all_gather(gate, "tp", axis=1, tiled=True),
    )
    updated_all = stream_all.astype(jnp.float32) + gate_all.astype(jnp.float32) * projected
    row_mean = jnp.mean(updated_all, axis=1, keepdims=True)
    row_var = jnp.mean(jnp.square(updated_all - row_mean), axis=1, keepdims=True)
    column = lax.axis_index("tp") * local_width
    updated = lax.dynamic_slice_in_dim(updated_all, column, local_width, 1)
    stream = updated.astype(jnp.bfloat16)
    normed = (
        (updated - row_mean) * lax.rsqrt(row_var + EPS) * (1.0 + scale.astype(jnp.float32))
        + shift.astype(jnp.float32)
    ).astype(jnp.bfloat16)
    return (stream, normed, cross_out)


def solution(mesh):
    in_specs = (
        P("req", "tp"),
        P("req", "tp"),
        P("req", "tp"),
        P("tp"),
        P("tp"),
        P("req", None, "tp"),
        P("req", None, "tp"),
        P("req", None),
        P("req"),
        P("req", None),
        P("req", None),
        P("req", "tp"),
        P("req", "tp"),
        P("req", "tp"),
        P("tp", "req"),
        P("req", "tp"),
        P("req", "tp"),
        P("req", "tp"),
        P("req", "tp"),
    )
    out_specs = (P("req", "tp"), P("req", "tp"), P("req", "tp"))
    return jax.shard_map(shards, mesh=mesh, in_specs=in_specs, out_specs=out_specs, check_vma=False)
```

profile of v0, /device:TPU:32, one launch (start us, length us, event | category | flops | bytes accessed | tf_op | source)
XLA Modules:
  0.0 377.1 jit_solution(8865713509482704299)
XLA Ops:
  11.3 18.4 %all-to-all-start.1 = ((bf16[64,2,8]{2,1,0:T(2,128)(2,1)}), bf16[64,2,8]{2,1,0:T(2,128)(2,1)S(1)}, u32[]{:S(2)}, u32[]{:S(2)}) async-start(bf16[64,2,8]{2,1,0:T(2,128)(2,1)} %broadcast_in_dim.15), calls=%async_computation.1 | async-start | bytes 65536 | tf_op jit(solution)/shard_map/all_to_all | solution.py:101
  31.7 1.3 copy.70
  33.0 10.6 %all-to-all-done.1 = bf16[64,2,8]{2,1,0:T(2,128)(2,1)S(1)} async-done(((bf16[64,2,8]{2,1,0:T(2,128)(2,1)}), bf16[64,2,8]{2,1,0:T(2,128)(2,1)S(1)}, u32[]{:S(2)}, u32[]{:S(2)}) %all-to-all-start.1) | async-done | bytes 2080 | tf_op jit(solution)/shard_map/all_to_all | solution.py:101
  43.5 5.5 %all-to-all-start.2 = ((bf16[128,8,640]{2,1,0:T(8,128)(2,1)}), bf16[128,8,640]{2,1,0:T(8,128)(2,1)S(1)}, u32[]{:S(2)}, u32[]{:S(2)}) async-start(bf16[128,8,640]{2,1,0:T(8,128)(2,1)} %bitcast.52), calls=%async_computation.2 | async-start | bytes 2621440 | tf_op jit(solution)/shard_map/all_to_all | solution.py:99
  49.1 1.9 gather_fusion.1
  51.7 1.3 copy.68
  53.0 63.7 %all-to-all-done.2 = bf16[128,8,640]{2,1,0:T(8,128)(2,1)S(1)} async-done(((bf16[128,8,640]{2,1,0:T(8,128)(2,1)}), bf16[128,8,640]{2,1,0:T(8,128)(2,1)S(1)}, u32[]{:S(2)}, u32[]{:S(2)}) %all-to-all-start.2) | async-done | bytes 1310752 | tf_op jit(solution)/shard_map/all_to_all | solution.py:99
  116.7 10.4 %all-to-all-start = ((bf16[128,8,640]{2,1,0:T(8,128)(2,1)}), bf16[128,8,640]{2,1,0:T(8,128)(2,1)}, u32[]{:S(2)}, u32[]{:S(2)}) async-start(bf16[128,8,640]{2,1,0:T(8,128)(2,1)} %bitcast.51), calls=%async_computation | async-start | bytes 2621440 | tf_op jit(solution)/shard_map/all_to_all | solution.py:100
  128.0 1.4 gather_fusion.2
  129.4 2.7 gather_fusion
  132.8 19.0 %all-reduce = (f32[256]{0:T(256)S(1)}, f32[256]{0:T(256)S(1)}) all-reduce(f32[256]{0:T(256)S(1)} %fusion.34, f32[256]{0:T(256)S(1)} %fusion.37), channel_id=1, replica_groups=mesh['req'=64,'tp'=8] {'tp'}, use_global_device_ids=true, to_apply=%region_4.0 | all-reduce | flops 512 | bytes 4096 | tf_op jit(solution)/shard_map/psum | solution.py:61
  151.9 0.9 copy.54
  153.5 1.6 concatenate.28
  156.0 1.6 concatenate.23
  157.6 1.2 copy.48
  158.8 1.9 copy.47
  160.7 1.9 fusion.36
  162.8 3.1 concatenate.29
  165.9 1.3 copy.53
  167.2 32.5 %all-to-all-done = bf16[128,8,640]{2,1,0:T(8,128)(2,1)} async-done(((bf16[128,8,640]{2,1,0:T(8,128)(2,1)}), bf16[128,8,640]{2,1,0:T(8,128)(2,1)}, u32[]{:S(2)}, u32[]{:S(2)}) %all-to-all-start) | async-done | bytes 1310752 | tf_op jit(solution)/shard_map/all_to_all | solution.py:100
  199.7 3.1 concatenate.24
  202.8 2.6 copy.49
  205.4 3.3 fusion
  208.7 1.9 fusion.1
  210.7 1.9 fusion.29
  212.6 6.7 %convolution_convert_fusion = bf16[256,5120]{1,0:T(8,128)(2,1)} fusion(bf16[256,640]{0,1:T(8,128)(2,1)S(1)} %bitcast.71, bf16[640,5120]{0,1:T(8,128)(2,1)} %all-gather.5.cloned.1.call-done), kind=kOutput, calls=%fused_computation.7 | convolution fusion | flops 1679032320 | bytes 9502720 | tf_op jit(solution)/shard_map/dot_general | solution.py:118
  219.3 28.4 %all_gather.10 = bf16[1,5120]{1,0:T(2,128)(2,1)S(1)} all-gather(bf16[1,640]{1,0:T(2,128)(2,1)S(1)} %copy-done.15), channel_id=1, replica_groups=mesh['req'=64,'tp'=8] {'tp'}, dimensions={1}, use_global_device_ids=true | all-gather | bytes 11520 | tf_op jit(solution)/shard_map/all_gather | solution.py:126
  249.0 0.9 copy.62
  249.9 11.1 %all-gather.3.cloned.1.call-done = bf16[256,5120]{1,0:T(8,128)(2,1)} async-done(((bf16[256,640]{1,0:T(8,128)(2,1)}), bf16[256,5120]{1,0:T(8,128)(2,1)}) %all-gather.3.cloned.1.call-update) | async-done | bytes 2621456 | tf_op jit(solution)/shard_map/all_gather | solution.py:125
  261.0 103.8 %all-reduce.3.cloned.1.call-done = bf16[256,5120]{1,0:T(8,128)(2,1)} async-done(((bf16[256,5120]{1,0:T(8,128)(2,1)}), bf16[256,5120]{1,0:T(8,128)(2,1)}) %all-reduce.3.cloned.1.call-update) | async-done | bytes 2621456 | tf_op jit(solution)/shard_map/psum | solution.py:123
  364.8 3.5 fusion.55
  369.7 0.9 add_convert_fusion
  (81 shorter events, 12.2 us)
Async XLA Ops:
  7.2 23.2 %copy-start = (bf16[112,8,640]{2,1,0:T(8,128)(2,1)S(1)}, bf16[112,8,640]{2,1,0:T(8,128)(2,1)}, u32[]{:S(2)}) copy-start(bf16[112,8,640]{2,1,0:T(8,128)(2,1)} %param.24) | copy-start | bytes 3440644
  7.2 205.4 %all-gather.5.cloned.1.call-start = ((), (), s32[]{:S(2)}) async-start(), calls=%async_computation.4 | async-start | bytes 6656000 | tf_op jit(solution)/shard_map/all_gather | solution.py:120
  11.3 32.3 %all-to-all-start.1 = ((bf16[64,2,8]{2,1,0:T(2,128)(2,1)}), bf16[64,2,8]{2,1,0:T(2,128)(2,1)S(1)}, u32[]{:S(2)}, u32[]{:S(2)}) async-start(bf16[64,2,8]{2,1,0:T(2,128)(2,1)} %broadcast_in_dim.15), calls=%async_computation.1 | async-start | bytes 65536 | tf_op jit(solution)/shard_map/all_to_all | solution.py:101
  43.5 73.2 %all-to-all-start.2 = ((bf16[128,8,640]{2,1,0:T(8,128)(2,1)}), bf16[128,8,640]{2,1,0:T(8,128)(2,1)S(1)}, u32[]{:S(2)}, u32[]{:S(2)}) async-start(bf16[128,8,640]{2,1,0:T(8,128)(2,1)} %bitcast.52), calls=%async_computation.2 | async-start | bytes 2621440 | tf_op jit(solution)/shard_map/all_to_all | solution.py:99
  51.0 77.0 %copy-start.16 = (s32[1,48]{1,0:T(1,128)S(1)}, s32[1,48]{1,0:T(1,128)}, u32[]{:S(2)}) copy-start(s32[1,48]{1,0:T(1,128)} %param.26) | copy-start | bytes 580
  51.7 80.4 %copy-start.5 = (bf16[256,640]{1,0:T(8,128)(2,1)S(1)}, bf16[256,640]{1,0:T(8,128)(2,1)}, u32[]{:S(2)}) copy-start(bf16[256,640]{1,0:T(8,128)(2,1)} %param.19) | copy-start | bytes 983044
  51.7 80.6 %copy-start.6 = (bf16[256,640]{1,0:T(8,128)(2,1)S(1)}, bf16[256,640]{1,0:T(8,128)(2,1)}, u32[]{:S(2)}) copy-start(bf16[256,640]{1,0:T(8,128)(2,1)} %param.20) | copy-start | bytes 983044
  51.7 100.0 %copy-start.11 = (f32[640]{0:T(1024)S(1)}, f32[640]{0:T(1024)}, u32[]{:S(2)}) copy-start(f32[640]{0:T(1024)} %param.23) | copy-start | bytes 7684
  116.7 38.4 %copy-start.1 = (bf16[128,8,640]{2,1,0:T(8,128)(2,1)}, bf16[128,8,640]{2,1,0:T(8,128)(2,1)S(1)}, u32[]{:S(2)}) copy-start(bf16[128,8,640]{2,1,0:T(8,128)(2,1)S(1)} %all-to-all-done.2) | copy-start | bytes 3932164
  116.7 83.0 %all-to-all-start = ((bf16[128,8,640]{2,1,0:T(8,128)(2,1)}), bf16[128,8,640]{2,1,0:T(8,128)(2,1)}, u32[]{:S(2)}, u32[]{:S(2)}) async-start(bf16[128,8,640]{2,1,0:T(8,128)(2,1)} %bitcast.51), calls=%async_computation | async-start | bytes 2621440 | tf_op jit(solution)/shard_map/all_to_all | solution.py:100
  127.2 133.9 %all-gather.3.cloned.1.call-start = ((), (), s32[]{:S(2)}) async-start(), calls=%async_computation.3 | async-start | bytes 2949120 | tf_op jit(solution)/shard_map/all_gather | solution.py:125
  127.9 236.9 %all-reduce.3.cloned.1.call-start = ((), (), s32[]{:S(2)}) async-start(), calls=%async_computation.5 | async-start | bytes 5242880 | tf_op jit(solution)/shard_map/psum | solution.py:123
  132.3 20.5 %copy-start.2 = (bf16[256,640]{0,1:T(8,128)(2,1)}, bf16[256,640]{0,1:T(8,128)(2,1)S(1)}, u32[]{:S(2)}) copy-start(bf16[256,640]{0,1:T(8,128)(2,1)S(1)} %copy.50) | copy-start | bytes 983044
  132.4 28.4 %copy-start.12 = (f32[640]{0:T(1024)S(1)}, f32[640]{0:T(1024)}, u32[]{:S(2)}) copy-start(f32[640]{0:T(1024)} %param.22) | copy-start | bytes 7684
  208.7 1.9 copy-start.3
  208.7 1.9 copy-start.4
  208.7 1.9 copy-start.8
  212.6 6.7 %copy-start.15 = (bf16[1,640]{1,0:T(2,128)(2,1)S(1)}, bf16[1,640]{1,0:T(2,128)(2,1)}, u32[]{:S(2)}) copy-start(bf16[1,640]{1,0:T(2,128)(2,1)} %param.35) | copy-start | bytes 3844
  212.6 35.2 %copy-start.7 = (bf16[256,640]{1,0:T(8,128)(2,1)S(1)}, bf16[256,640]{1,0:T(8,128)(2,1)}, u32[]{:S(2)}) copy-start(bf16[256,640]{1,0:T(8,128)(2,1)} %param.30) | copy-start | bytes 983044
  212.6 35.4 %copy-start.9 = (bf16[128,640]{1,0:T(8,128)(2,1)S(1)}, bf16[128,640]{1,0:T(8,128)(2,1)}, u32[]{:S(2)}) copy-start(bf16[128,640]{1,0:T(8,128)(2,1)} %param.31) | copy-start | bytes 491524
  212.6 35.5 %copy-start.10 = (bf16[128,640]{1,0:T(8,128)(2,1)S(1)}, bf16[128,640]{1,0:T(8,128)(2,1)}, u32[]{:S(2)}) copy-start(bf16[128,640]{1,0:T(8,128)(2,1)} %param.32) | copy-start | bytes 491524
  219.3 30.7 %copy-start.13 = (bf16[1,640]{1,0:T(2,128)(2,1)S(1)}, bf16[1,640]{1,0:T(2,128)(2,1)}, u32[]{:S(2)}) copy-start(bf16[1,640]{1,0:T(2,128)(2,1)} %param.36) | copy-start | bytes 3844
  219.3 30.7 %copy-start.14 = (bf16[1,640]{1,0:T(2,128)(2,1)S(1)}, bf16[1,640]{1,0:T(2,128)(2,1)}, u32[]{:S(2)}) copy-start(bf16[1,640]{1,0:T(2,128)(2,1)} %param.37) | copy-start | bytes 3844
Sparse Core Ops, SparseCore 0:
  11.0 198.7 all-gather.4
  211.9 49.0 all-gather.2
  264.0 100.7 all-reduce.2
where the time goes:
time: 378 us; the launch traced here: 377 us
  waiting for transfers between devices  223 us (59%)
  blocking collectives  47.4 us (13%)
  starting transfers between devices  34.5 us (9%)
  local copies, waits for them, and re-layouts  31.3 us (8%)
  between operations  14.8 us (4%)
  matrix products  13.6 us (4%)
  other arithmetic  12.5 us (3%)
    psum x1, waiting for transfers between devices, shards(): lax.psum(partial_rows.astype(jnp.bfloat16), 'tp').astype(jnp.float32)  104 us
    all_to_all x1, waiting for transfers between devices, shards(): lax.all_to_all(sent_keys, 'req', split_axis=0, concat_axis=0, tiled=True)  63.7 us
    all_to_all x1, waiting for transfers between devices, shards(): lax.all_to_all(sent_values, 'req', split_axis=0, concat_axis=0, tiled=True)  32.5 us
    all_gather x1, blocking collectives, shards(): lax.all_gather(gate, 'tp', axis=1, tiled=True)  28.4 us
    psum x1, blocking collectives, shards(): lax.psum((jnp.sum(query_float * query_float, axis=1), jnp.sum(key_float *...  19 us
    all_to_all x1, starting transfers between devices, shards(): lax.all_to_all(sent_flags, 'req', split_axis=0, concat_axis=0, tiled=True)  18.4 us
    all_gather x1, waiting for transfers between devices, shards(): lax.all_gather(residual, 'tp', axis=1, tiled=True)  11.1 us
    all_to_all x1, waiting for transfers between devices, shards(): lax.all_to_all(sent_flags, 'req', split_axis=0, concat_axis=0, tiled=True)  10.6 us
  transfers between devices with their start and end apart: 6, of which 5 were waited for; matrix products, arithmetic and copies ran while one was open for 14% of the time, Pallas kernels for 0%

commit v1 on v0

v1 whole, which is shorter than its diff:
```python
import math

import jax
import jax.numpy as jnp
from jax import lax
from jax.experimental import pallas as pl
from jax.experimental.pallas import tpu as pltpu
from jax.sharding import PartitionSpec as P

HD = 128
CAP = 2


EPS = 1e-06


def head_scores(query, keys, scale):
    return (
        lax.dot_general(query, keys, (((1,), (1,)), ((), ())), preferred_element_type=jnp.float32)
        * scale
    )


def self_kernel(q_ref, kr_ref, vr_ref, ka_ref, va_ref, kn_ref, vn_ref, ur_ref, ua_ref, o_ref):
    scale = 1.0 / math.sqrt(HD)
    query = q_ref[...]
    resident = jnp.where(ur_ref[...] > 0, head_scores(query, kr_ref[...], scale), -jnp.inf)
    arrived = jnp.where(ua_ref[...] > 0, head_scores(query, ka_ref[...], scale), -jnp.inf)
    own = head_scores(query, kn_ref[...], scale)
    row_max = jnp.maximum(
        jnp.max(own, axis=1, keepdims=True),
        jnp.maximum(
            jnp.max(resident, axis=1, keepdims=True), jnp.max(arrived, axis=1, keepdims=True)
        ),
    )
    denominator = jnp.zeros_like(row_max)
    mixed = jnp.zeros(o_ref.shape, jnp.float32)
    for scores, values in ((resident, vr_ref), (arrived, va_ref), (own, vn_ref)):
        exponent = jnp.exp(scores - row_max)
        denominator += jnp.sum(exponent, axis=1, keepdims=True)
        mixed += jnp.dot(
            exponent.astype(jnp.bfloat16), values[...], preferred_element_type=jnp.float32
        )
    o_ref[...] = (mixed / denominator).astype(jnp.bfloat16)


def cross_kernel(q_ref, k_ref, v_ref, o_ref):
    scores = head_scores(q_ref[...], k_ref[...], 1.0 / math.sqrt(HD))
    exponent = jnp.exp(scores - jnp.max(scores, axis=1, keepdims=True))
    denominator = jnp.sum(exponent, axis=1, keepdims=True)
    mixed = jnp.dot(exponent.astype(jnp.bfloat16), v_ref[...], preferred_element_type=jnp.float32)
    o_ref[...] = (mixed / denominator).astype(jnp.bfloat16)


def per_head(kernel, rows, masks, width):
    spec = lambda array: pl.BlockSpec((array.shape[0], HD), lambda h: (0, h))
    flag = lambda array: pl.BlockSpec(array.shape, lambda h: (0, 0))
    keys = sum(array.shape[0] for array in rows[1:]) // 2
    tokens = rows[0].shape[0]
    return pl.pallas_call(
        kernel,
        grid=(width // HD,),
        out_shape=jax.ShapeDtypeStruct((tokens, width), jnp.bfloat16),
        in_specs=[spec(array) for array in rows] + [flag(array) for array in masks],
        out_specs=pl.BlockSpec((tokens, HD), lambda h: (0, h)),
        cost_estimate=pl.CostEstimate(
            flops=4 * tokens * keys * width,
            bytes_accessed=4 * (tokens + keys) * width,
            transcendentals=tokens * keys * width // HD,
        ),
    )(*rows, *masks)


def shards(
    queries,
    new_keys,
    new_values,
    query_gain,
    key_gain,
    cache_keys,
    cache_values,
    page_table,
    cache_lens,
    mig_pages,
    mig_dest,
    cross_queries,
    text_keys,
    text_values,
    out_weight,
    residual,
    gate,
    shift,
    scale,
):
    token_count, local_width = queries.shape
    tp_count = lax.axis_size("tp")
    full_width = local_width * tp_count
    peer_count = lax.axis_size("req")
    page_len = cache_keys.shape[1]
    peers = jnp.arange(peer_count, dtype=jnp.int32)

    destination = mig_dest[:, 0]
    slot_match = (destination[:, None] == peers[None, :]).astype(jnp.int32)
    position = jnp.sum(jnp.cumsum(slot_match, axis=0) * slot_match, axis=1) - 1
    target_slot = destination * CAP + position
    selection = jnp.arange(peer_count * CAP, dtype=jnp.int32)[:, None] == target_slot[None, :]
    slot_page = jnp.sum(jnp.where(selection, mig_pages, 0), axis=1)
    sent_keys = cache_keys[slot_page]
    sent_values = cache_values[slot_page]
    arrived_keys = lax.all_to_all(sent_keys, "req", split_axis=0, concat_axis=0, tiled=True)
    arrived_values = lax.all_to_all(sent_values, "req", split_axis=0, concat_axis=0, tiled=True)

    all_dest = lax.all_gather(mig_dest, "req", axis=1, tiled=True)
    arrivals = jnp.sum((all_dest == lax.axis_index("req")).astype(jnp.int32), axis=0)
    filled = arrivals[:, None] > jnp.arange(CAP, dtype=jnp.int32)[None, :]
    arrived_usable = jnp.broadcast_to(
        filled[:, :, None].astype(jnp.float32), (peer_count, CAP, page_len)
    ).reshape(1, -1)

    query_float = queries.astype(jnp.float32)
    key_float = new_keys.astype(jnp.float32)
    query_squares, key_squares = lax.psum(
        (jnp.sum(query_float * query_float, axis=1), jnp.sum(key_float * key_float, axis=1)), "tp"
    )
    query_normed = (
        query_float * lax.rsqrt(query_squares / full_width + EPS)[:, None] * query_gain
    ).astype(jnp.bfloat16)
    key_normed = (key_float * lax.rsqrt(key_squares / full_width + EPS)[:, None] * key_gain).astype(
        jnp.bfloat16
    )
    own_pages = page_table[0]
    resident_keys = cache_keys[own_pages].reshape(-1, local_width)
    resident_values = cache_values[own_pages].reshape(-1, local_width)
    resident_usable = (
        jnp.arange(resident_keys.shape[0], dtype=jnp.int32) < cache_lens[0]
    ).astype(jnp.float32)[None, :]

    cross_out = per_head(cross_kernel, (cross_queries, text_keys, text_values), (), local_width)
    attended = per_head(
        self_kernel,
        (
            query_normed,
            resident_keys,
            resident_values,
            arrived_keys.reshape(-1, local_width),
            arrived_values.reshape(-1, local_width),
            key_normed,
            new_values,
        ),
        (resident_usable, arrived_usable),
        local_width,
    )
    whole_weight = lax.all_gather(out_weight, "req", axis=1, tiled=True)
    partial_rows = jnp.dot(attended, whole_weight, preferred_element_type=jnp.float32).astype(
        jnp.bfloat16
    )
    pieces = lax.all_to_all(
        jnp.stack(jnp.split(partial_rows, tp_count, axis=1)),
        "tp",
        split_axis=0,
        concat_axis=0,
        tiled=True,
    )
    projected = jnp.sum(pieces.astype(jnp.float32), axis=0)
    updated = residual.astype(jnp.float32) + gate.astype(jnp.float32) * projected
    local_mean = jnp.mean(updated, axis=1)
    local_var = jnp.mean(jnp.square(updated - local_mean[:, None]), axis=1)
    means, variances = lax.all_gather(jnp.stack([local_mean, local_var]), "tp", axis=1)
    row_mean = jnp.mean(means, axis=0)
    row_var = jnp.mean(variances + jnp.square(means - row_mean[None, :]), axis=0)
    stream = updated.astype(jnp.bfloat16)
    normed = (
        (updated - row_mean[:, None])
        * lax.rsqrt(row_var + EPS)[:, None]
        * (1.0 + scale.astype(jnp.float32))
        + shift.astype(jnp.float32)
    ).astype(jnp.bfloat16)
    return (stream, normed, cross_out)


def solution(mesh):
    in_specs = (
        P("req", "tp"),
        P("req", "tp"),
        P("req", "tp"),
        P("tp"),
        P("tp"),
        P("req", None, "tp"),
        P("req", None, "tp"),
        P("req", None),
        P("req"),
        P("req", None),
        P("req", None),
        P("req", "tp"),
        P("req", "tp"),
        P("req", "tp"),
        P("tp", "req"),
        P("req", "tp"),
        P("req", "tp"),
        P("req", "tp"),
        P("req", "tp"),
    )
    out_specs = (P("req", "tp"), P("req", "tp"), P("req", "tp"))
    return jax.shard_map(shards, mesh=mesh, in_specs=in_specs, out_specs=out_specs, check_vma=False)
```

time: 378 us -> 360 us (0.952)
  the two profiles are of different devices: /device:TPU:32 before, /device:TPU:8 now
where the time goes in v1:
time: 360 us; the launch traced here: 359 us
  blocking collectives  174 us (48%)
  waiting for transfers between devices  92.8 us (26%)
  starting transfers between devices  32.6 us (9%)
  local copies, waits for them, and re-layouts  16.2 us (4%)
  between operations  14.9 us (4%)
  Pallas kernels  11.8 us (3%)
  other arithmetic  11.4 us (3%)
  matrix products  5.21 us (1%)
    all_gather x1, blocking collectives, shards(): all_dest = lax.all_gather(mig_dest, 'req', axis=1, tiled=True)  130 us
    all_to_all x1, waiting for transfers between devices, shards(): lax.all_to_all(sent_keys, 'req', split_axis=0, concat_axis=0, tiled=True)  68.5 us
    all_gather x1, blocking collectives, shards(): lax.all_gather(jnp.stack([local_mean, local_var]), 'tp', axis=1)  24.1 us
    all_to_all x1, waiting for transfers between devices, shards(): lax.all_to_all(jnp.stack(jnp.split(partial_rows, tp_count, axis=1)), 'tp'...  23.6 us
    psum x1, blocking collectives, shards(): lax.psum((jnp.sum(query_float * query_float, axis=1), jnp.sum(key_float *...  19.4 us
    all_to_all x1, starting transfers between devices, shards(): lax.all_to_all(sent_keys, 'req', split_axis=0, concat_axis=0, tiled=True)  17.8 us
    pallas_call x2, Pallas kernels, per_head(): pl.pallas_call(kernel, grid=(width // HD,), out_shape=jax.ShapeDtypeStruc...  11.8 us
    all_to_all x1, starting transfers between devices, shards(): lax.all_to_all(sent_values, 'req', split_axis=0, concat_axis=0, tiled=True)  9.42 us
  transfers between devices with their start and end apart: 4, of which 2 were waited for; matrix products, arithmetic and copies ran while one was open for 5% of the time, Pallas kernels for 3%

profile of v1, /device:TPU:8, one launch (start us, length us, event | category | flops | bytes accessed | tf_op | source)
XLA Modules:
  0.0 358.8 jit_solution(10140485421767238761)
XLA Ops:
  7.9 0.7 fusion.15
  8.7 0.8 select_reduce_fusion.1
  10.2 0.7 select_reduce_fusion
  11.7 1.9 gather_fusion.2
  13.6 17.8 %all-to-all-start = ((bf16[128,8,640]{2,1,0:T(8,128)(2,1)}), bf16[128,8,640]{2,1,0:T(8,128)(2,1)S(1)}, u32[]{:S(2)}, u32[]{:S(2)}) async-start(bf16[128,8,640]{2,1,0:T(8,128)(2,1)} %gather_fusion.2), calls=%async_computation | async-start | bytes 2621440 | tf_op jit(solution)/shard_map/all_to_all | solution.py:110
  31.4 3.1 gather_fusion.3
  34.5 68.5 %all-to-all-done = bf16[128,8,640]{2,1,0:T(8,128)(2,1)S(1)} async-done(((bf16[128,8,640]{2,1,0:T(8,128)(2,1)}), bf16[128,8,640]{2,1,0:T(8,128)(2,1)S(1)}, u32[]{:S(2)}, u32[]{:S(2)}) %all-to-all-start) | async-done | bytes 1310752 | tf_op jit(solution)/shard_map/all_to_all | solution.py:110
  103.0 9.4 %all-to-all-start.1 = ((bf16[128,8,640]{2,1,0:T(8,128)(2,1)}), bf16[128,8,640]{2,1,0:T(8,128)(2,1)}, u32[]{:S(2)}, u32[]{:S(2)}) async-start(bf16[128,8,640]{2,1,0:T(8,128)(2,1)} %gather_fusion.3), calls=%async_computation.1 | async-start | bytes 2621440 | tf_op jit(solution)/shard_map/all_to_all | solution.py:111
  112.4 1.4 gather_fusion
  113.9 2.7 gather_fusion.1
  116.6 130.4 %all-gather.1 = s32[64,1,64]{2,1,0:T(1,128)S(1)} all-gather(s32[1,1,64]{2,1,0:T(1,128)S(1)} %bitcast.60), channel_id=1, replica_groups=mesh['req'=64,'tp'=8] {'req'}, dimensions={0}, use_global_device_ids=true | all-gather | bytes 16640 | tf_op jit(solution)/shard_map/all_gather | solution.py:113
  247.0 1.2 fusion.14
  248.5 0.7 reshape.144.ua_ref
  250.2 19.4 %all-reduce = (f32[256]{0:T(256)S(1)}, f32[256]{0:T(256)S(1)}) all-reduce(f32[256]{0:T(256)S(1)} %fusion, f32[256]{0:T(256)S(1)} %fusion.3), channel_id=1, replica_groups=mesh['req'=64,'tp'=8] {'tp'}, use_global_device_ids=true, to_apply=%region_1.2 | all-reduce | flops 512 | bytes 4096 | tf_op jit(solution)/shard_map/psum | solution.py:122
  270.2 0.9 fusion.2.q_ref
  271.0 0.9 fusion.5.kn_ref
  271.9 7.3 %shard_map.202 = bf16[256,640]{1,0:T(8,128)(2,1)} custom-call(bf16[256,640]{1,0:T(8,128)(2,1)} %fusion.2.q_ref, bf16[384,640]{1,0:T(8,128)(2,1)} %bitcast.55, bf16[384,640]{1,0:T(8,128)(2,1)} %bitcast.56, bf16[1024,640]{1,0:T(8,128)(2,1)} %bitcast.54, bf16[1024,640]{1,0:T(8,128)(2,1)} %bitcast.9.va_ref, bf16[256,640]{1,0:T(8,128)(2,1)} %fusion.5.kn_ref, ...), custom_call_target="tpu_custom_call" | custom-call | flops 1090519040 | bytes 4915200 | tf_op jit(solution)/shard_map/pallas_call | solution.py:60
  279.2 5.2 %convolution_convert_fusion = bf16[256,5120]{1,0:T(8,128)(2,1)S(1)} fusion(bf16[256,640]{1,0:T(8,128)(2,1)} %shard_map.202, bf16[640,5120]{0,1:T(8,128)(2,1)} %all-gather.4.cloned.1.call-done), kind=kOutput, calls=%fused_computation.4 | convolution fusion | flops 1679032320 | bytes 9502720 | tf_op jit(solution)/shard_map/dot_general | solution.py:154
  284.5 0.8 fusion.13
  285.2 0.8 fusion.12
  286.0 0.8 fusion.11
  286.8 0.8 fusion.10
  287.5 0.8 fusion.9
  288.3 0.8 fusion.8
  289.0 0.8 fusion.7
  289.8 0.8 fusion.6
  290.6 5.3 %all-to-all-start.2 = ((bf16[8,256,640]{2,1,0:T(8,128)(2,1)}), bf16[8,256,640]{2,1,0:T(8,128)(2,1)}, u32[]{:S(2)}, u32[]{:S(2)}) async-start(bf16[8,256,640]{2,1,0:T(8,128)(2,1)} %fusion.6), calls=%async_computation.2 | async-start | bytes 5242880 | tf_op jit(solution)/shard_map/all_to_all | solution.py:157
  295.9 4.5 %shard_map.203 = bf16[256,640]{1,0:T(8,128)(2,1)} custom-call(bf16[256,640]{1,0:T(8,128)(2,1)} %q_ref.1, bf16[128,640]{1,0:T(8,128)(2,1)} %k_ref.1, bf16[128,640]{1,0:T(8,128)(2,1)} %v_ref.1), custom_call_target="tpu_custom_call" | custom-call | flops 83886080 | bytes 983040 | tf_op jit(solution)/shard_map/pallas_call | solution.py:60
  300.4 23.6 %all-to-all-done.2 = bf16[8,256,640]{2,1,0:T(8,128)(2,1)} async-done(((bf16[8,256,640]{2,1,0:T(8,128)(2,1)}), bf16[8,256,640]{2,1,0:T(8,128)(2,1)}, u32[]{:S(2)}, u32[]{:S(2)}) %all-to-all-start.2) | async-done | bytes 2621472 | tf_op jit(solution)/shard_map/all_to_all | solution.py:157
  324.1 2.2 convert_reduce_fusion
  326.7 24.1 %all-gather = f32[2,2048]{1,0:T(2,128)S(1)} all-gather(f32[2,256]{1,0:T(2,128)S(1)} %pad_maximum_fusion), channel_id=2, replica_groups=mesh['req'=64,'tp'=8] {'tp'}, dimensions={1}, use_global_device_ids=true | all-gather | bytes 18432 | tf_op jit(solution)/shard_map/all_gather | solution.py:168
  350.9 1.0 add_convert_fusion
  (51 shorter events, 3.9 us)
Async XLA Ops:
  7.2 4.5 %copy-start = (bf16[112,8,640]{2,1,0:T(8,128)(2,1)S(1)}, bf16[112,8,640]{2,1,0:T(8,128)(2,1)}, u32[]{:S(2)}) copy-start(bf16[112,8,640]{2,1,0:T(8,128)(2,1)} %param.24) | copy-start | bytes 3440644
  7.2 272.1 %all-gather.4.cloned.1.call-start = ((), (), s32[]{:S(2)}) async-start(), calls=%async_computation.3 | async-start | bytes 6656000 | tf_op jit(solution)/shard_map/all_gather | solution.py:153
  13.6 89.4 %all-to-all-start = ((bf16[128,8,640]{2,1,0:T(8,128)(2,1)}), bf16[128,8,640]{2,1,0:T(8,128)(2,1)S(1)}, u32[]{:S(2)}, u32[]{:S(2)}) async-start(bf16[128,8,640]{2,1,0:T(8,128)(2,1)} %gather_fusion.2), calls=%async_computation | async-start | bytes 2621440 | tf_op jit(solution)/shard_map/all_to_all | solution.py:110
  34.5 82.1 %copy-start.5 = (s32[64,1]{0,1:T(1,128)S(1)}, s32[64,1]{0,1:T(1,128)}, u32[]{:S(2)}) copy-start(s32[64,1]{0,1:T(1,128)} %param.29) | copy-start | bytes 772
  34.5 215.4 %copy-start.3 = (bf16[256,640]{1,0:T(8,128)(2,1)S(1)}, bf16[256,640]{1,0:T(8,128)(2,1)}, u32[]{:S(2)}) copy-start(bf16[256,640]{1,0:T(8,128)(2,1)} %param.19) | copy-start | bytes 983044
  34.5 215.5 %copy-start.4 = (bf16[256,640]{1,0:T(8,128)(2,1)S(1)}, bf16[256,640]{1,0:T(8,128)(2,1)}, u32[]{:S(2)}) copy-start(bf16[256,640]{1,0:T(8,128)(2,1)} %param.20) | copy-start | bytes 983044
  34.5 235.7 %copy-start.6 = (f32[640]{0:T(1024)S(1)}, f32[640]{0:T(1024)}, u32[]{:S(2)}) copy-start(f32[640]{0:T(1024)} %param.22) | copy-start | bytes 7684
  34.5 236.6 %copy-start.7 = (f32[640]{0:T(1024)S(1)}, f32[640]{0:T(1024)}, u32[]{:S(2)}) copy-start(f32[640]{0:T(1024)} %param.23) | copy-start | bytes 7684
  103.0 147.1 %copy-start.1 = (bf16[128,8,640]{2,1,0:T(8,128)(2,1)}, bf16[128,8,640]{2,1,0:T(8,128)(2,1)S(1)}, u32[]{:S(2)}) copy-start(bf16[128,8,640]{2,1,0:T(8,128)(2,1)S(1)} %all-to-all-done) | copy-start | bytes 3932164
  103.0 168.9 %all-to-all-start.1 = ((bf16[128,8,640]{2,1,0:T(8,128)(2,1)}), bf16[128,8,640]{2,1,0:T(8,128)(2,1)}, u32[]{:S(2)}, u32[]{:S(2)}) async-start(bf16[128,8,640]{2,1,0:T(8,128)(2,1)} %gather_fusion.3), calls=%async_computation.1 | async-start | bytes 2621440 | tf_op jit(solution)/shard_map/all_to_all | solution.py:111
  290.6 9.8 %copy-start.8 = (bf16[1,640]{1,0:T(2,128)(2,1)S(1)}, bf16[1,640]{1,0:T(2,128)(2,1)}, u32[]{:S(2)}) copy-start(bf16[1,640]{1,0:T(2,128)(2,1)} %param.37) | copy-start | bytes 3844
  290.6 9.8 %copy-start.9 = (bf16[1,640]{1,0:T(2,128)(2,1)S(1)}, bf16[1,640]{1,0:T(2,128)(2,1)}, u32[]{:S(2)}) copy-start(bf16[1,640]{1,0:T(2,128)(2,1)} %param.36) | copy-start | bytes 3844
  290.6 9.8 %copy-start.10 = (bf16[1,640]{1,0:T(2,128)(2,1)S(1)}, bf16[1,640]{1,0:T(2,128)(2,1)}, u32[]{:S(2)}) copy-start(bf16[1,640]{1,0:T(2,128)(2,1)} %param.35) | copy-start | bytes 3844
  290.6 33.5 %all-to-all-start.2 = ((bf16[8,256,640]{2,1,0:T(8,128)(2,1)}), bf16[8,256,640]{2,1,0:T(8,128)(2,1)}, u32[]{:S(2)}, u32[]{:S(2)}) async-start(bf16[8,256,640]{2,1,0:T(8,128)(2,1)} %fusion.6), calls=%async_computation.2 | async-start | bytes 5242880 | tf_op jit(solution)/shard_map/all_to_all | solution.py:157
  295.9 30.4 %copy-start.2 = (bf16[256,640]{1,0:T(8,128)(2,1)S(1)}, bf16[256,640]{1,0:T(8,128)(2,1)}, u32[]{:S(2)}) copy-start(bf16[256,640]{1,0:T(8,128)(2,1)} %param.34) | copy-start | bytes 983044
Sparse Core Ops, SparseCore 0:
  11.0 198.3 all-gather.3

commit v2 on v1

--- a/solution.py
+++ b/solution.py
@@ -1,3 +1,4 @@
+import functools
 import math
 
 import jax
@@ -69,6 +70,211 @@
             transcendentals=tokens * keys * width // HD,
         ),
     )(*rows, *masks)
+
+
+MESH = pl.DeviceIdType.MESH
+
+
+def exchange_kernel(
+    layers,
+    key_ref,
+    value_ref,
+    count_ref,
+    square_ref,
+    weight_ref,
+    key_out,
+    value_out,
+    count_out,
+    square_out,
+    weight_out,
+    page_send,
+    page_recv,
+    tp_send,
+    tp_recv,
+    local_sem,
+    right_recv,
+    left_recv,
+    row_recv,
+    core_recv,
+    weight_send,
+):
+    peer_count = 4 * layers
+    req, tp = lax.axis_index("req"), lax.axis_index("tp")
+    tp_count = square_out.shape[0]
+    half, layer, core = req // (2 * layers), (req // 2) % layers, req % 2
+
+    def place(h, z, c):
+        return (h * layers + z) * 2 + c
+
+    barrier = pltpu.get_barrier_semaphore()
+
+    @pl.loop(1, peer_count)
+    def _(i):
+        pl.semaphore_signal(
+            barrier, inc=1, device_id=((req + i) % peer_count, tp), device_id_type=MESH
+        )
+
+    @pl.loop(1, tp_count)
+    def _(i):
+        pl.semaphore_signal(
+            barrier, inc=1, device_id=(req, (tp + i) % tp_count), device_id_type=MESH
+        )
+
+    locals_ = [
+        pltpu.make_async_copy(key_ref.at[req], key_out.at[req], local_sem.at[0]),
+        pltpu.make_async_copy(value_ref.at[req], value_out.at[req], local_sem.at[1]),
+        pltpu.make_async_copy(count_ref.at[req], count_out.at[req], local_sem.at[2]),
+        pltpu.make_async_copy(square_ref, square_out.at[tp], local_sem.at[3]),
+        pltpu.make_async_copy(weight_ref, weight_out.at[req], local_sem.at[4]),
+    ]
+    for copy in locals_:
+        copy.start()
+    pl.semaphore_wait(barrier, peer_count + tp_count - 2)
+
+    @pl.loop(1, tp_count)
+    def _(i):
+        pltpu.make_async_remote_copy(
+            src_ref=square_ref,
+            dst_ref=square_out.at[tp],
+            send_sem=tp_send,
+            recv_sem=tp_recv,
+            device_id=(req, (tp + i) % tp_count),
+            device_id_type=MESH,
+        ).start()
+
+    def send_weight(source, origin, target, recv_sem):
+        pltpu.make_async_remote_copy(
+            src_ref=source,
+            dst_ref=weight_out.at[origin],
+            send_sem=weight_send,
+            recv_sem=recv_sem,
+            device_id=(target, tp),
+            device_id_type=MESH,
+        ).start()
+
+    def wait_block(sem):
+        pltpu.make_async_copy(weight_out.at[0], weight_out.at[0], sem).wait()
+
+    right = place(half, (layer + 1) % layers, core)
+    left = place(half, (layer + layers - 1) % layers, core)
+    across = place((half + 1) % 2, layer, core)
+    beside = place(half, layer, (core + 1) % 2)
+
+    def send_pages(target):
+        for src, dst, sem in (
+            (key_ref, key_out, 0),
+            (value_ref, value_out, 1),
+            (count_ref, count_out, 2),
+        ):
+            pltpu.make_async_remote_copy(
+                src_ref=src.at[target],
+                dst_ref=dst.at[req],
+                send_sem=page_send.at[sem],
+                recv_sem=page_recv.at[sem],
+                device_id=(target, tp),
+                device_id_type=MESH,
+            ).start()
+
+    def batch(k):
+        shift = layers // 2 - (k + 1) // 2
+        z = (layer + layers + shift * (2 * (k % 2) - 1)) % layers
+        for h in range(2):
+            for c in range(2):
+                send_pages(place((half + h) % 2, z, (core + c) % 2))
+
+    send_weight(weight_ref, req, right, right_recv.at[0])
+    send_weight(weight_ref, req, left, left_recv.at[0])
+    send_weight(weight_ref, req, across, row_recv.at[layer])
+    send_weight(weight_ref, req, beside, core_recv)
+    right_steps = layers // 2
+    left_steps = layers - 1 - right_steps
+    batch(0)
+
+    def step(s, from_left, from_right):
+        if from_left is not None:
+            z = (layer + layers - 1 - s) % layers
+            origin = place(half, z, core)
+            wait_block(right_recv.at[s])
+            if from_left:
+                send_weight(weight_out.at[origin], origin, right, right_recv.at[s + 1])
+            send_weight(weight_out.at[origin], origin, across, row_recv.at[z])
+            send_weight(weight_out.at[origin], origin, beside, core_recv)
+        if from_right is not None:
+            z = (layer + 1 + s) % layers
+            origin = place(half, z, core)
+            wait_block(left_recv.at[s])
+            if from_right:
+                send_weight(weight_out.at[origin], origin, left, left_recv.at[s + 1])
+            send_weight(weight_out.at[origin], origin, across, row_recv.at[z])
+            send_weight(weight_out.at[origin], origin, beside, core_recv)
+        batch(s + 1)
+
+    @pl.loop(0, left_steps - 1)
+    def _(s):
+        step(s, True, True)
+
+    for s in range(left_steps - 1, right_steps):
+        step(s, s < right_steps - 1, s < left_steps - 1 if s < left_steps else None)
+
+    @pl.loop(right_steps + 1, layers - 1)
+    def _(k):
+        batch(k)
+
+    for h, c in ((0, 1), (1, 0), (1, 1)):
+        send_pages(place((half + h) % 2, layer, (core + c) % 2))
+
+    @pl.loop(0, layers)
+    def _(s):
+        z = (layer + layers + ((s + 1) // 2) * (2 * (s % 2) - 1)) % layers
+        origin = place((half + 1) % 2, z, core)
+        wait_block(row_recv.at[z])
+        send_weight(weight_out.at[origin], origin, beside, core_recv)
+
+    for copy in locals_:
+        copy.wait()
+    halves = weight_out.at[pl.ds(0, 2 * layers)]
+    pltpu.make_async_copy(halves, halves, core_recv).wait()
+    sent = weight_out.at[pl.ds(0, 4 * layers - 1)]
+    pltpu.make_async_copy(sent, sent, weight_send).wait()
+    for sem, out in ((0, key_out), (1, value_out), (2, count_out)):
+        others = out.at[pl.ds(0, peer_count - 1)]
+        pltpu.make_async_copy(others, others, page_recv.at[sem]).wait()
+        pltpu.make_async_copy(others, others, page_send.at[sem]).wait()
+    others = square_out.at[pl.ds(0, tp_count - 1)]
+    pltpu.make_async_copy(others, others, tp_recv).wait()
+    pltpu.make_async_copy(others, others, tp_send).wait()
+
+
+def exchange(keys, values, counts, squares, weight, tp_count):
+    peer_count = keys.shape[0]
+    layers = peer_count // 4
+    anywhere = pl.BlockSpec(memory_space=pl.ANY)
+    shape = jax.ShapeDtypeStruct
+    return pl.pallas_call(
+        functools.partial(exchange_kernel, layers),
+        out_shape=(
+            shape(keys.shape, keys.dtype),
+            shape(values.shape, values.dtype),
+            shape(counts.shape, counts.dtype),
+            shape((tp_count,) + squares.shape, squares.dtype),
+            shape((peer_count,) + weight.shape, weight.dtype),
+        ),
+        in_specs=[anywhere] * 5,
+        out_specs=(anywhere,) * 5,
+        scratch_shapes=[
+            pltpu.SemaphoreType.DMA((3,)),
+            pltpu.SemaphoreType.DMA((3,)),
+            pltpu.SemaphoreType.DMA,
+            pltpu.SemaphoreType.DMA,
+            pltpu.SemaphoreType.DMA((5,)),
+            pltpu.SemaphoreType.DMA((layers,)),
+            pltpu.SemaphoreType.DMA((layers,)),
+            pltpu.SemaphoreType.DMA((layers,)),
+            pltpu.SemaphoreType.DMA,
+            pltpu.SemaphoreType.DMA,
+        ],
+        compiler_params=pltpu.CompilerParams(collective_id=0, has_side_effects=True),
+    )(keys, values, counts, squares, weight)
 
 
 def shards(
@@ -105,23 +311,24 @@
     target_slot = destination * CAP + position
     selection = jnp.arange(peer_count * CAP, dtype=jnp.int32)[:, None] == target_slot[None, :]
     slot_page = jnp.sum(jnp.where(selection, mig_pages, 0), axis=1)
-    sent_keys = cache_keys[slot_page]
-    sent_values = cache_values[slot_page]
-    arrived_keys = lax.all_to_all(sent_keys, "req", split_axis=0, concat_axis=0, tiled=True)
-    arrived_values = lax.all_to_all(sent_values, "req", split_axis=0, concat_axis=0, tiled=True)
-
-    all_dest = lax.all_gather(mig_dest, "req", axis=1, tiled=True)
-    arrivals = jnp.sum((all_dest == lax.axis_index("req")).astype(jnp.int32), axis=0)
-    filled = arrivals[:, None] > jnp.arange(CAP, dtype=jnp.int32)[None, :]
+    sent_keys = cache_keys[slot_page].reshape(peer_count, CAP * page_len, local_width)
+    sent_values = cache_values[slot_page].reshape(peer_count, CAP * page_len, local_width)
+    sent_counts = jnp.broadcast_to(
+        jnp.sum(slot_match, axis=0)[:, None, None], (peer_count, 1, HD)
+    )
+    query_float = queries.astype(jnp.float32)
+    key_float = new_keys.astype(jnp.float32)
+    local_squares = jnp.stack(
+        [jnp.sum(query_float * query_float, axis=1), jnp.sum(key_float * key_float, axis=1)]
+    )
+    arrived_keys, arrived_values, arrivals, all_squares, whole_weight = exchange(
+        sent_keys, sent_values, sent_counts, local_squares[:, None, :], out_weight.T, tp_count
+    )
+    filled = arrivals[:, 0, :1] > jnp.arange(CAP, dtype=jnp.int32)[None, :]
     arrived_usable = jnp.broadcast_to(
         filled[:, :, None].astype(jnp.float32), (peer_count, CAP, page_len)
     ).reshape(1, -1)
-
-    query_float = queries.astype(jnp.float32)
-    key_float = new_keys.astype(jnp.float32)
-    query_squares, key_squares = lax.psum(
-        (jnp.sum(query_float * query_float, axis=1), jnp.sum(key_float * key_float, axis=1)), "tp"
-    )
+    query_squares, key_squares = jnp.sum(all_squares[:, :, 0, :], axis=0)
     query_normed = (
         query_float * lax.rsqrt(query_squares / full_width + EPS)[:, None] * query_gain
     ).astype(jnp.bfloat16)
@@ -150,10 +357,12 @@
         (resident_usable, arrived_usable),
         local_width,
     )
-    whole_weight = lax.all_gather(out_weight, "req", axis=1, tiled=True)
-    partial_rows = jnp.dot(attended, whole_weight, preferred_element_type=jnp.float32).astype(
-        jnp.bfloat16
-    )
+    partial_rows = lax.dot_general(
+        attended,
+        whole_weight.reshape(full_width, local_width),
+        (((1,), (1,)), ((), ())),
+        preferred_element_type=jnp.float32,
+    ).astype(jnp.bfloat16)
     pieces = lax.all_to_all(
         jnp.stack(jnp.split(partial_rows, tp_count, axis=1)),
         "tp",

time: 360 us -> 274 us (0.76)
  the two profiles are of different devices: /device:TPU:8 before, /device:TPU:50 now
where the time goes in v2:
time: 274 us; the launch traced here: 273 us
  Pallas kernels  175 us (64%)
  waiting for transfers between devices  32.2 us (12%)
  blocking collectives  25.7 us (9%)
  local copies, waits for them, and re-layouts  16.9 us (6%)
  other arithmetic  11.1 us (4%)
  starting transfers between devices  5.67 us (2%)
  matrix products  5.21 us (2%)
    pallas_call x1, Pallas kernels, exchange(): pl.pallas_call(functools.partial(exchange_kernel, layers), out_shape=(sha...  163 us
    all_to_all x1, waiting for transfers between devices, shards(): lax.all_to_all(jnp.stack(jnp.split(partial_rows, tp_count, axis=1)), 'tp'...  32.2 us
    all_gather x1, blocking collectives, shards(): lax.all_gather(jnp.stack([local_mean, local_var]), 'tp', axis=1)  25.7 us
    pallas_call x2, Pallas kernels, per_head(): pl.pallas_call(kernel, grid=(width // HD,), out_shape=jax.ShapeDtypeStruc...  11.8 us
    all_to_all x1, starting transfers between devices, shards(): lax.all_to_all(jnp.stack(jnp.split(partial_rows, tp_count, axis=1)), 'tp'...  5.67 us
  transfers between devices with their start and end apart: 1, of which 1 were waited for; matrix products, arithmetic and copies ran while one was open for 0% of the time, Pallas kernels for 2%

profile of v2, /device:TPU:50, one launch (start us, length us, event | category | flops | bytes accessed | tf_op | source)
XLA Modules:
  0.0 272.8 jit_solution(16070882232193294593)
XLA Ops:
  0.7 0.9 fusion.14
  1.6 0.8 fusion.16
  2.5 0.7 add_add_fusion
  3.2 0.7 select_reduce_fusion
  3.9 0.7 fusion.22
  4.6 1.8 gather_fusion
  6.4 1.8 gather_fusion.1
  8.2 1.4 gather_fusion.2
  9.6 1.4 gather_fusion.3
  11.9 0.7 broadcast_in_dim.23.count_ref
  12.7 162.7 %shard_map.202 = (bf16[64,16,640]{2,1,0:T(8,128)(2,1)}, bf16[64,16,640]{2,1,0:T(8,128)(2,1)}, s32[64,1,128]{2,1,0:T(1,128)}, f32[8,2,1,256]{3,2,1,0:T(1,128)}, bf16[64,80,640]{2,1,0:T(8,128)(2,1)}) custom-call(bf16[64,16,640]{2,1,0:T(8,128)(2,1)} %bitcast.61, bf16[64,16,640]{2,1,0:T(8,128)(2,1)} %bitcast.62, s32[64,1,128]{2,1,0:T(1,128)} %broadcast_in_dim.23.count_ref, ...), custom_call_target="tpu_custom_call" | custom-call | tf_op jit(solution)/shard_map/pallas_call | solution.py:253
  175.4 0.7 reduce_sum.107
  176.2 2.0 slice_reduce_fusion
  178.4 0.7 reshape.183.ua_ref
  180.4 0.9 fusion.2.q_ref
  181.2 0.9 fusion.5.kn_ref
  182.1 7.3 %shard_map.203 = bf16[256,640]{1,0:T(8,128)(2,1)} custom-call(bf16[256,640]{1,0:T(8,128)(2,1)} %fusion.2.q_ref, bf16[384,640]{1,0:T(8,128)(2,1)} %bitcast.63, bf16[384,640]{1,0:T(8,128)(2,1)} %bitcast.64, bf16[1024,640]{1,0:T(8,128)(2,1)} %bitcast.65, bf16[1024,640]{1,0:T(8,128)(2,1)} %bitcast.66, bf16[256,640]{1,0:T(8,128)(2,1)} %fusion.5.kn_ref, ...), custom_call_target="tpu_custom_call" | custom-call | flops 1090519040 | bytes 4915200 | tf_op jit(solution)/shard_map/pallas_call | solution.py:61
  189.5 5.2 %convolution_convert_fusion = bf16[256,5120]{1,0:T(8,128)(2,1)S(1)} fusion(bf16[256,640]{1,0:T(8,128)(2,1)} %shard_map.203, bf16[5120,640]{1,0:T(8,128)(2,1)} %bitcast.76), kind=kOutput, calls=%fused_computation.4 | convolution fusion | flops 1679032320 | bytes 9502720 | tf_op jit(solution)/shard_map/dot_general | solution.py:360
  194.7 0.8 fusion.13
  195.4 0.8 fusion.12
  196.2 0.8 fusion.11
  197.0 0.8 fusion.10
  197.7 0.8 fusion.9
  198.5 0.8 fusion.8
  199.2 0.8 fusion.7
  200.0 0.8 fusion.6
  200.8 5.7 %all-to-all-start = ((bf16[8,256,640]{2,1,0:T(8,128)(2,1)}), bf16[8,256,640]{2,1,0:T(8,128)(2,1)}, u32[]{:S(2)}, u32[]{:S(2)}) async-start(bf16[8,256,640]{2,1,0:T(8,128)(2,1)} %fusion.6), calls=%async_computation | async-start | bytes 5242880 | tf_op jit(solution)/shard_map/all_to_all | solution.py:366
  206.5 4.5 %shard_map.204 = bf16[256,640]{1,0:T(8,128)(2,1)} custom-call(bf16[256,640]{1,0:T(8,128)(2,1)} %q_ref.1, bf16[128,640]{1,0:T(8,128)(2,1)} %k_ref.1, bf16[128,640]{1,0:T(8,128)(2,1)} %v_ref.1), custom_call_target="tpu_custom_call" | custom-call | flops 83886080 | bytes 983040 | tf_op jit(solution)/shard_map/pallas_call | solution.py:61
  211.0 32.2 %all-to-all-done = bf16[8,256,640]{2,1,0:T(8,128)(2,1)} async-done(((bf16[8,256,640]{2,1,0:T(8,128)(2,1)}), bf16[8,256,640]{2,1,0:T(8,128)(2,1)}, u32[]{:S(2)}, u32[]{:S(2)}) %all-to-all-start) | async-done | bytes 2621472 | tf_op jit(solution)/shard_map/all_to_all | solution.py:366
  243.2 2.2 convert_reduce_fusion
  245.8 25.7 %all-gather = f32[2,2048]{1,0:T(2,128)S(1)} all-gather(f32[2,256]{1,0:T(2,128)S(1)} %pad_maximum_fusion.1), channel_id=2, replica_groups=mesh['req'=64,'tp'=8] {'tp'}, dimensions={1}, use_global_device_ids=true | all-gather | bytes 18432 | tf_op jit(solution)/shard_map/all_gather | solution.py:377
  271.7 1.0 add_convert_fusion
  (45 shorter events, 2.4 us)
Async XLA Ops:
  0.6 4.0 %copy-start = (bf16[112,8,640]{2,1,0:T(8,128)(2,1)S(1)}, bf16[112,8,640]{2,1,0:T(8,128)(2,1)}, u32[]{:S(2)}) copy-start(bf16[112,8,640]{2,1,0:T(8,128)(2,1)} %param.24) | copy-start | bytes 3440644
  0.6 5.7 %copy-start.2 = (bf16[112,8,640]{2,1,0:T(8,128)(2,1)S(1)}, bf16[112,8,640]{2,1,0:T(8,128)(2,1)}, u32[]{:S(2)}) copy-start(bf16[112,8,640]{2,1,0:T(8,128)(2,1)} %param.25) | copy-start | bytes 3440644
  6.4 4.7 %copy-start.3 = (bf16[256,640]{1,0:T(8,128)(2,1)S(1)}, bf16[256,640]{1,0:T(8,128)(2,1)}, u32[]{:S(2)}) copy-start(bf16[256,640]{1,0:T(8,128)(2,1)} %param.19) | copy-start | bytes 983044
  6.4 4.8 %copy-start.4 = (bf16[256,640]{1,0:T(8,128)(2,1)S(1)}, bf16[256,640]{1,0:T(8,128)(2,1)}, u32[]{:S(2)}) copy-start(bf16[256,640]{1,0:T(8,128)(2,1)} %param.20) | copy-start | bytes 983044
  8.2 172.2 %copy-start.5 = (f32[640]{0:T(1024)S(1)}, f32[640]{0:T(1024)}, u32[]{:S(2)}) copy-start(f32[640]{0:T(1024)} %param.22) | copy-start | bytes 7684
  9.6 171.6 %copy-start.6 = (f32[640]{0:T(1024)S(1)}, f32[640]{0:T(1024)}, u32[]{:S(2)}) copy-start(f32[640]{0:T(1024)} %param.23) | copy-start | bytes 7684
  200.8 10.2 %copy-start.7 = (bf16[1,640]{1,0:T(2,128)(2,1)S(1)}, bf16[1,640]{1,0:T(2,128)(2,1)}, u32[]{:S(2)}) copy-start(bf16[1,640]{1,0:T(2,128)(2,1)} %param.37) | copy-start | bytes 3844
  200.8 10.2 %copy-start.8 = (bf16[1,640]{1,0:T(2,128)(2,1)S(1)}, bf16[1,640]{1,0:T(2,128)(2,1)}, u32[]{:S(2)}) copy-start(bf16[1,640]{1,0:T(2,128)(2,1)} %param.36) | copy-start | bytes 3844
  200.8 10.2 %copy-start.9 = (bf16[1,640]{1,0:T(2,128)(2,1)S(1)}, bf16[1,640]{1,0:T(2,128)(2,1)}, u32[]{:S(2)}) copy-start(bf16[1,640]{1,0:T(2,128)(2,1)} %param.35) | copy-start | bytes 3844
  200.8 42.4 %all-to-all-start = ((bf16[8,256,640]{2,1,0:T(8,128)(2,1)}), bf16[8,256,640]{2,1,0:T(8,128)(2,1)}, u32[]{:S(2)}, u32[]{:S(2)}) async-start(bf16[8,256,640]{2,1,0:T(8,128)(2,1)} %fusion.6), calls=%async_computation | async-start | bytes 5242880 | tf_op jit(solution)/shard_map/all_to_all | solution.py:366
  206.5 38.9 %copy-start.1 = (bf16[256,640]{1,0:T(8,128)(2,1)S(1)}, bf16[256,640]{1,0:T(8,128)(2,1)}, u32[]{:S(2)}) copy-start(bf16[256,640]{1,0:T(8,128)(2,1)} %param.34) | copy-start | bytes 983044

commit v3 on v2

--- a/solution.py
+++ b/solution.py
@@ -82,11 +82,15 @@
     count_ref,
     square_ref,
     weight_ref,
+    cross_query_ref,
+    text_key_ref,
+    text_value_ref,
     key_out,
     value_out,
     count_out,
     square_out,
     weight_out,
+    cross_ref,
     page_send,
     page_recv,
     tp_send,
@@ -230,6 +234,15 @@
         wait_block(row_recv.at[z])
         send_weight(weight_out.at[origin], origin, beside, core_recv)
 
+    for head in range(cross_ref.shape[1] // HD):
+        columns = pl.ds(head * HD, HD)
+        cross_kernel(
+            cross_query_ref.at[:, columns],
+            text_key_ref.at[:, columns],
+            text_value_ref.at[:, columns],
+            cross_ref.at[:, columns],
+        )
+
     for copy in locals_:
         copy.wait()
     halves = weight_out.at[pl.ds(0, 2 * layers)]
@@ -245,10 +258,11 @@
     pltpu.make_async_copy(others, others, tp_send).wait()
 
 
-def exchange(keys, values, counts, squares, weight, tp_count):
+def exchange(keys, values, counts, squares, weight, cross, tp_count):
     peer_count = keys.shape[0]
     layers = peer_count // 4
     anywhere = pl.BlockSpec(memory_space=pl.ANY)
+    vmem = pl.BlockSpec(memory_space=pltpu.VMEM)
     shape = jax.ShapeDtypeStruct
     return pl.pallas_call(
         functools.partial(exchange_kernel, layers),
@@ -258,9 +272,10 @@
             shape(counts.shape, counts.dtype),
             shape((tp_count,) + squares.shape, squares.dtype),
             shape((peer_count,) + weight.shape, weight.dtype),
+            shape(cross[0].shape, cross[0].dtype),
         ),
-        in_specs=[anywhere] * 5,
-        out_specs=(anywhere,) * 5,
+        in_specs=[anywhere] * 5 + [vmem] * 3,
+        out_specs=(anywhere,) * 5 + (vmem,),
         scratch_shapes=[
             pltpu.SemaphoreType.DMA((3,)),
             pltpu.SemaphoreType.DMA((3,)),
@@ -274,7 +289,194 @@
             pltpu.SemaphoreType.DMA,
         ],
         compiler_params=pltpu.CompilerParams(collective_id=0, has_side_effects=True),
-    )(keys, values, counts, squares, weight)
+    )(keys, values, counts, squares, weight, *cross)
+
+
+def project_kernel(
+    attended_ref,
+    weight_ref,
+    residual_ref,
+    gate_ref,
+    shift_ref,
+    scale_ref,
+    stream_ref,
+    normed_ref,
+    far,
+    to_right,
+    to_left,
+    relay_right,
+    relay_left,
+    from_left,
+    from_right,
+    own,
+    to_row,
+    from_row,
+    stat_out,
+    stat_in,
+    send_sem,
+    recv_sem,
+    stat_sem,
+):
+    req, tp = lax.axis_index("req"), lax.axis_index("tp")
+    tp_count = stat_in.shape[0]
+    ring = tp_count // 2
+    row, x = tp // ring, tp % ring
+    tokens, width = residual_ref.shape
+    part = tokens // 2
+
+    barrier = pltpu.get_barrier_semaphore()
+    for i in range(1, tp_count):
+        pl.semaphore_signal(
+            barrier, inc=1, device_id=(req, (tp + i) % tp_count), device_id_type=MESH
+        )
+
+    right = row * ring + (x + 1) % ring
+    left = row * ring + (x + ring - 1) % ring
+    other = ((row + 1) % 2) * ring + x
+
+    def send(src, dst, sem, target):
+        copy = pltpu.make_async_remote_copy(
+            src_ref=src,
+            dst_ref=dst,
+            send_sem=send_sem.at[sem],
+            recv_sem=recv_sem.at[sem],
+            device_id=(req, target),
+            device_id_type=MESH,
+        )
+        copy.start()
+        return copy
+
+    def block(shift, j):
+        owner = ((row + j) % 2) * ring + (x + shift) % ring
+        rows = weight_ref[pl.ds(pl.multiple_of(owner * width, width), width), :]
+        return lax.dot_general(
+            attended_ref[...],
+            rows,
+            (((1,), (1,)), ((), ())),
+            preferred_element_type=jnp.float32,
+        ).astype(jnp.bfloat16)
+
+    for j in range(2):
+        product = block(2, j)
+        for p in range(2):
+            far[p, j] = product[p * part : (p + 1) * part]
+    pl.semaphore_wait(barrier, tp_count - 1)
+    copies = [send(far.at[0], relay_right, 0, right), send(far.at[1], relay_left, 1, left)]
+    for j in range(2):
+        product = block(1, j)
+        for p in range(2):
+            to_right[p, j] = product[p * part : (p + 1) * part]
+    copies.append(send(to_right.at[1], from_left.at[1], 2, right))
+    for j in range(2):
+        product = block(ring - 1, j)
+        for p in range(2):
+            to_left[p, j] = product[p * part : (p + 1) * part]
+    copies.append(send(to_left.at[0], from_right.at[0], 3, left))
+    for j in range(2):
+        product = block(0, j)
+        for p in range(2):
+            own[p, j] = product[p * part : (p + 1) * part]
+
+    def total(*terms):
+        return functools.reduce(jnp.add, [term.astype(jnp.float32) for term in terms])
+
+    copies[0].wait_recv()
+    for j in range(2):
+        to_right[0, j] = total(to_right[0, j], relay_right[j]).astype(jnp.bfloat16)
+    copies.append(send(to_right.at[0], from_left.at[0], 4, right))
+    copies[1].wait_recv()
+    for j in range(2):
+        to_left[1, j] = total(to_left[1, j], relay_left[j]).astype(jnp.bfloat16)
+    copies.append(send(to_left.at[1], from_right.at[1], 5, left))
+    copies[2].wait_recv()
+    copies[3].wait_recv()
+    for p in range(2):
+        copies[4 + p].wait_recv()
+        to_row[p] = total(own[p, 1], from_left[p, 1], from_right[p, 1]).astype(jnp.bfloat16)
+        copies.append(send(to_row.at[p], from_row.at[p], 6 + p, other))
+
+    updated = []
+    for p in range(2):
+        local = total(own[p, 0], from_left[p, 0], from_right[p, 0])
+        copies[6 + p].wait_recv()
+        span = pl.ds(p * part, part)
+        value = residual_ref[span, :].astype(jnp.float32) + gate_ref[...].astype(jnp.float32) * (
+            local + from_row[p].astype(jnp.float32)
+        )
+        stream_ref[span, :] = value.astype(jnp.bfloat16)
+        mean = jnp.sum(value, axis=1, keepdims=True) / width
+        variance = jnp.sum(jnp.square(value - mean), axis=1, keepdims=True) / width
+        lane = lax.broadcasted_iota(jnp.int32, (part, HD), 1)
+        packed = jnp.where(lane == 0, mean, jnp.where(lane == 1, variance, 0.0))
+        stat_out[p] = jnp.transpose(packed)[0:8]
+        updated.append(value)
+
+    stat_in[tp] = stat_out[...]
+    for i in range(1, tp_count):
+        copy = pltpu.make_async_remote_copy(
+            src_ref=stat_out,
+            dst_ref=stat_in.at[tp],
+            send_sem=stat_sem.at[0],
+            recv_sem=stat_sem.at[1],
+            device_id=(req, (tp + i) % tp_count),
+            device_id_type=MESH,
+        )
+        copy.start()
+    others = stat_in.at[pl.ds(0, tp_count - 1)]
+    pltpu.make_async_copy(others, others, stat_sem.at[1]).wait()
+    for p in range(2):
+        arrived = [stat_in[i, p] for i in range(tp_count)]
+        row_mean = functools.reduce(jnp.add, [a[0:1] for a in arrived]) / tp_count
+        row_var = (
+            functools.reduce(
+                jnp.add, [a[1:2] + jnp.square(a[0:1] - row_mean) for a in arrived]
+            )
+            / tp_count
+        )
+        line = lax.broadcasted_iota(jnp.int32, (HD, part), 0)
+        packed = jnp.transpose(
+            jnp.where(line == 0, row_mean, jnp.where(line == 1, lax.rsqrt(row_var + EPS), 0.0))
+        )
+        normed = (updated[p] - packed[:, 0:1]) * packed[:, 1:2] * (
+            1.0 + scale_ref[...].astype(jnp.float32)
+        ) + shift_ref[...].astype(jnp.float32)
+        normed_ref[pl.ds(p * part, part), :] = normed.astype(jnp.bfloat16)
+    for copy in copies:
+        copy.wait_send()
+    pltpu.make_async_copy(others, others, stat_sem.at[0]).wait()
+
+
+def project(attended, weight, residual, gate, shift, scale, tp_count):
+    tokens, width = residual.shape
+    part = tokens // 2
+    vmem = pl.BlockSpec(memory_space=pltpu.VMEM)
+    pair = pltpu.VMEM((2, part, width), jnp.bfloat16)
+    quad = pltpu.VMEM((2, 2, part, width), jnp.bfloat16)
+    stat = pltpu.VMEM((2, 8, part), jnp.float32)
+    return pl.pallas_call(
+        project_kernel,
+        out_shape=(jax.ShapeDtypeStruct(residual.shape, jnp.bfloat16),) * 2,
+        in_specs=[vmem] * 6,
+        out_specs=(vmem, vmem),
+        scratch_shapes=[
+            quad,
+            quad,
+            quad,
+            pair,
+            pair,
+            quad,
+            quad,
+            quad,
+            pair,
+            pair,
+            stat,
+            pltpu.VMEM((tp_count, 2, 8, part), jnp.float32),
+            pltpu.SemaphoreType.DMA((8,)),
+            pltpu.SemaphoreType.DMA((8,)),
+            pltpu.SemaphoreType.DMA((2,)),
+        ],
+        compiler_params=pltpu.CompilerParams(collective_id=1, has_side_effects=True),
+    )(attended, weight, residual, gate, shift, scale)
 
 
 def shards(
@@ -321,8 +523,14 @@
     local_squares = jnp.stack(
         [jnp.sum(query_float * query_float, axis=1), jnp.sum(key_float * key_float, axis=1)]
     )
-    arrived_keys, arrived_values, arrivals, all_squares, whole_weight = exchange(
-        sent_keys, sent_values, sent_counts, local_squares[:, None, :], out_weight.T, tp_count
+    arrived_keys, arrived_values, arrivals, all_squares, whole_weight, cross_out = exchange(
+        sent_keys,
+        sent_values,
+        sent_counts,
+        local_squares[:, None, :],
+        out_weight.T,
+        (cross_queries, text_keys, text_values),
+        tp_count,
     )
     filled = arrivals[:, 0, :1] > jnp.arange(CAP, dtype=jnp.int32)[None, :]
     arrived_usable = jnp.broadcast_to(
@@ -342,7 +550,6 @@
         jnp.arange(resident_keys.shape[0], dtype=jnp.int32) < cache_lens[0]
     ).astype(jnp.float32)[None, :]
 
-    cross_out = per_head(cross_kernel, (cross_queries, text_keys, text_values), (), local_width)
     attended = per_head(
         self_kernel,
         (
@@ -357,33 +564,15 @@
         (resident_usable, arrived_usable),
         local_width,
     )
-    partial_rows = lax.dot_general(
+    stream, normed = project(
         attended,
         whole_weight.reshape(full_width, local_width),
-        (((1,), (1,)), ((), ())),
-        preferred_element_type=jnp.float32,
-    ).astype(jnp.bfloat16)
-    pieces = lax.all_to_all(
-        jnp.stack(jnp.split(partial_rows, tp_count, axis=1)),
-        "tp",
-        split_axis=0,
-        concat_axis=0,
-        tiled=True,
-    )
-    projected = jnp.sum(pieces.astype(jnp.float32), axis=0)
-    updated = residual.astype(jnp.float32) + gate.astype(jnp.float32) * projected
-    local_mean = jnp.mean(updated, axis=1)
-    local_var = jnp.mean(jnp.square(updated - local_mean[:, None]), axis=1)
-    means, variances = lax.all_gather(jnp.stack([local_mean, local_var]), "tp", axis=1)
-    row_mean = jnp.mean(means, axis=0)
-    row_var = jnp.mean(variances + jnp.square(means - row_mean[None, :]), axis=0)
-    stream = updated.astype(jnp.bfloat16)
-    normed = (
-        (updated - row_mean[:, None])
-        * lax.rsqrt(row_var + EPS)[:, None]
-        * (1.0 + scale.astype(jnp.float32))
-        + shift.astype(jnp.float32)
-    ).astype(jnp.bfloat16)
+        residual,
+        gate,
+        shift,
+        scale,
+        tp_count,
+    )
     return (stream, normed, cross_out)
 
 

time: 274 us -> 238 us (0.87)
  the two profiles are of different devices: /device:TPU:50 before, /device:TPU:32 now
where the time goes in v3:
time: 238 us; the launch traced here: 237 us
  Pallas kernels  216 us (91%)
  local copies, waits for them, and re-layouts  14.2 us (6%)
  other arithmetic  5.98 us (3%)
    pallas_call x1, Pallas kernels, exchange(): pl.pallas_call(functools.partial(exchange_kernel, layers), out_shape=(sha...  163 us
    pallas_call x1, Pallas kernels, project(): pl.pallas_call(project_kernel, out_shape=(jax.ShapeDtypeStruct(residual.s...  45.2 us
    pallas_call x1, Pallas kernels, per_head(): pl.pallas_call(kernel, grid=(width // HD,), out_shape=jax.ShapeDtypeStruc...  7.32 us

profile of v3, /device:TPU:32, one launch (start us, length us, event | category | flops | bytes accessed | tf_op | source)
XLA Modules:
  0.0 237.1 jit_solution(5155067475518053597)
XLA Ops:
  0.6 0.0 copy-start
  0.6 0.8 fusion.6
  1.5 0.1 reduce_window_sum.11
  1.6 0.8 fusion.8
  2.4 0.7 add_add_fusion
  3.1 0.7 select_reduce_fusion
  3.9 0.0 copy-done
  3.9 0.0 copy-start.1
  3.9 1.8 gather_fusion
  5.7 0.0 copy-done.1
  5.7 1.8 gather_fusion.1
  7.5 0.7 broadcast_in_dim.23.count_ref
  8.2 0.1 fusion
  8.4 0.1 fusion.3
  8.5 0.6 broadcast_in_dim.24.square_ref
  9.1 163.0 %shard_map.202 = (bf16[64,16,640]{2,1,0:T(8,128)(2,1)}, bf16[64,16,640]{2,1,0:T(8,128)(2,1)}, s32[64,1,128]{2,1,0:T(1,128)}, f32[8,2,1,256]{3,2,1,0:T(1,128)}, b...) custom-call(bf16[64,16,640]{2,1,0:T(8,128)(2,1)} %bitcast.26, bf16[64,16,640]{2,1,0:T(8,128)(2,1)} %bitcast.27, ...), custom_call_target="tpu_custom_call" | custom-call | tf_op jit(solution)/shard_map/pallas_call | solution.py:267
  172.1 0.0 copy-start.5
  172.1 0.0 copy-start.8
  172.1 0.8 reduce_sum.62
  172.9 1.1 fusion.2
  174.0 1.3 slice_reduce_fusion
  175.2 0.1 fusion.7
  175.3 0.1 broadcast_in_dim.25
  175.5 0.7 reshape.151.ua_ref
  176.2 1.5 gather_fusion.2
  177.7 1.4 gather_fusion.3
  179.8 0.6 compare_convert_fusion.ur_ref
  180.3 7.3 %shard_map.203.attended_ref = bf16[256,640]{1,0:T(8,128)(2,1)} custom-call(bf16[256,640]{1,0:T(8,128)(2,1)} %get-tuple-element.23.q_ref, bf16[384,640]{1,0:T(8,128)(2,1)} %bitcast.28, bf16[384,640]{1,0:T(8,128)(2,1)} %bitcast.29, bf16[1024,640]{1,0:T(8,128)(2,1)} %bitcast.30, bf16[1024,640]{1,0:T(8,128)(2,1)} %bitcast.31, ...), custom_call_target="tpu_custom_call" | custom-call | flops 1090519040 | bytes 4915200 | tf_op jit(solution)/shard_map/pallas_call | solution.py:61
  187.7 45.2 %shard_map.204 = (bf16[256,640]{1,0:T(8,128)(2,1)}, bf16[256,640]{1,0:T(8,128)(2,1)}) custom-call(bf16[256,640]{1,0:T(8,128)(2,1)} %shard_map.203.attended_ref, bf16[5120,640]{1,0:T(8,128)(2,1)} %bitcast.25, bf16[256,640]{1,0:T(8,128)(2,1)} %residual_ref.1, bf16[1,640]{1,0:T(2,128)(2,1)} %gate_ref.1, bf16[1,640]{1,0:T(2,128)(2,1)} %shift_ref.1, ...), custom_call_target="tpu_custom_call" | custom-call | tf_op jit(solution)/shard_map/pallas_call | solution.py:456
  232.9 1.8 copy.26
  234.7 1.7 copy.27
  236.4 0.7 copy.28
  (18 shorter events, 0.1 us)
Async XLA Ops:
  0.6 3.2 %copy-start = (bf16[112,8,640]{2,1,0:T(8,128)(2,1)S(1)}, bf16[112,8,640]{2,1,0:T(8,128)(2,1)}, u32[]{:S(2)}) copy-start(bf16[112,8,640]{2,1,0:T(8,128)(2,1)} %param.24) | copy-start | bytes 3440644
  3.9 1.8 copy-start.1
  5.7 2.6 %copy-start.2 = (bf16[256,640]{1,0:T(8,128)(2,1)S(1)}, bf16[256,640]{1,0:T(8,128)(2,1)}, u32[]{:S(2)}) copy-start(bf16[256,640]{1,0:T(8,128)(2,1)} %param.19) | copy-start | bytes 983044
  5.7 2.7 %copy-start.3 = (bf16[256,640]{1,0:T(8,128)(2,1)S(1)}, bf16[256,640]{1,0:T(8,128)(2,1)}, u32[]{:S(2)}) copy-start(bf16[256,640]{1,0:T(8,128)(2,1)} %param.20) | copy-start | bytes 983044
  9.1 163.8 %copy-start.6 = (f32[640]{0:T(1024)S(1)}, f32[640]{0:T(1024)}, u32[]{:S(2)}) copy-start(f32[640]{0:T(1024)} %param.22) | copy-start | bytes 7684
  9.1 163.8 %copy-start.7 = (f32[640]{0:T(1024)S(1)}, f32[640]{0:T(1024)}, u32[]{:S(2)}) copy-start(f32[640]{0:T(1024)} %param.23) | copy-start | bytes 7684
  172.1 1.9 copy-start.5
  172.1 4.1 %copy-start.8 = (s32[1,48]{1,0:T(1,128)S(1)}, s32[1,48]{1,0:T(1,128)}, u32[]{:S(2)}) copy-start(s32[1,48]{1,0:T(1,128)} %param.26) | copy-start | bytes 580
  232.9 3.5 %copy-start.4 = (bf16[256,640]{1,0:T(8,128)(2,1)S(1)}, bf16[256,640]{1,0:T(8,128)(2,1)}, u32[]{:S(2)}) copy-start(bf16[256,640]{1,0:T(8,128)(2,1)} %get-tuple-element.30) | copy-start | bytes 983044

commit v4 on v3

--- a/solution.py
+++ b/solution.py
@@ -101,6 +101,9 @@
     row_recv,
     core_recv,
     weight_send,
+    relay,
+    relay_send,
+    relay_recv,
 ):
     peer_count = 4 * layers
     req, tp = lax.axis_index("req"), lax.axis_index("tp")
@@ -164,12 +167,11 @@
     across = place((half + 1) % 2, layer, core)
     beside = place(half, layer, (core + 1) % 2)
 
-    def send_pages(target):
-        for src, dst, sem in (
-            (key_ref, key_out, 0),
-            (value_ref, value_out, 1),
-            (count_ref, count_out, 2),
-        ):
+    pages = ((key_ref, key_out, 0), (value_ref, value_out, 1))
+    counts = (count_ref, count_out, 2)
+
+    def send_pages(target, what):
+        for src, dst, sem in what:
             pltpu.make_async_remote_copy(
                 src_ref=src.at[target],
                 dst_ref=dst.at[req],
@@ -184,7 +186,39 @@
         z = (layer + layers + shift * (2 * (k % 2) - 1)) % layers
         for h in range(2):
             for c in range(2):
-                send_pages(place((half + h) % 2, z, (core + c) % 2))
+                send_pages(place((half + h) % 2, z, (core + c) % 2), (*pages, counts))
+
+    opposite = (layer + layers // 2) % layers
+    quarter = layers // 4
+
+    def relayed(h):
+        target = place((half + h) % 2, opposite, (core + 1) % 2)
+        middle = place((half + h) % 2, (layer + layers - quarter) % layers, core)
+        send_pages(target, (counts,))
+        return [
+            pltpu.make_async_remote_copy(
+                src_ref=src.at[target],
+                dst_ref=relay.at[h, sem],
+                send_sem=relay_send.at[h, sem],
+                recv_sem=relay_recv.at[h, sem],
+                device_id=(middle, tp),
+                device_id_type=MESH,
+            )
+            for src, _, sem in pages
+        ]
+
+    def pass_on(h):
+        source = place((half + h) % 2, (layer + quarter) % layers, core)
+        target = place(half, (layer + layers - quarter) % layers, (core + 1) % 2)
+        for _, dst, sem in pages:
+            pltpu.make_async_remote_copy(
+                src_ref=relay.at[h, sem],
+                dst_ref=dst.at[source],
+                send_sem=page_send.at[sem],
+                recv_sem=page_recv.at[sem],
+                device_id=(target, tp),
+                device_id_type=MESH,
+            ).start()
 
     send_weight(weight_ref, req, right, right_recv.at[0])
     send_weight(weight_ref, req, left, left_recv.at[0])
@@ -192,7 +226,11 @@
     send_weight(weight_ref, req, beside, core_recv)
     right_steps = layers // 2
     left_steps = layers - 1 - right_steps
-    batch(0)
+    via = relayed(0) + relayed(1)
+    for copy in via:
+        copy.start()
+    for h in range(2):
+        send_pages(place((half + h) % 2, opposite, core), (*pages, counts))
 
     def step(s, from_left, from_right):
         if from_left is not None:
@@ -220,12 +258,17 @@
     for s in range(left_steps - 1, right_steps):
         step(s, s < right_steps - 1, s < left_steps - 1 if s < left_steps else None)
 
+    for copy in via:
+        copy.wait_recv()
+    for h in range(2):
+        pass_on(h)
+
     @pl.loop(right_steps + 1, layers - 1)
     def _(k):
         batch(k)
 
     for h, c in ((0, 1), (1, 0), (1, 1)):
-        send_pages(place((half + h) % 2, layer, (core + c) % 2))
+        send_pages(place((half + h) % 2, layer, (core + c) % 2), (*pages, counts))
 
     @pl.loop(0, layers)
     def _(s):
@@ -253,6 +296,8 @@
         others = out.at[pl.ds(0, peer_count - 1)]
         pltpu.make_async_copy(others, others, page_recv.at[sem]).wait()
         pltpu.make_async_copy(others, others, page_send.at[sem]).wait()
+    for copy in via:
+        copy.wait_send()
     others = square_out.at[pl.ds(0, tp_count - 1)]
     pltpu.make_async_copy(others, others, tp_recv).wait()
     pltpu.make_async_copy(others, others, tp_send).wait()
@@ -287,6 +332,9 @@
             pltpu.SemaphoreType.DMA((layers,)),
             pltpu.SemaphoreType.DMA,
             pltpu.SemaphoreType.DMA,
+            pltpu.VMEM((2, 2) + keys.shape[1:], keys.dtype),
+            pltpu.SemaphoreType.DMA((2, 2)),
+            pltpu.SemaphoreType.DMA((2, 2)),
         ],
         compiler_params=pltpu.CompilerParams(collective_id=0, has_side_effects=True),
     )(keys, values, counts, squares, weight, *cross)
@@ -297,10 +345,8 @@
     weight_ref,
     residual_ref,
     gate_ref,
-    shift_ref,
-    scale_ref,
-    stream_ref,
-    normed_ref,
+    updated_ref,
+    stat_ref,
     far,
     to_right,
     to_left,
@@ -395,7 +441,6 @@
         to_row[p] = total(own[p, 1], from_left[p, 1], from_right[p, 1]).astype(jnp.bfloat16)
         copies.append(send(to_row.at[p], from_row.at[p], 6 + p, other))
 
-    updated = []
     for p in range(2):
         local = total(own[p, 0], from_left[p, 0], from_right[p, 0])
         copies[6 + p].wait_recv()
@@ -403,13 +448,12 @@
         value = residual_ref[span, :].astype(jnp.float32) + gate_ref[...].astype(jnp.float32) * (
             local + from_row[p].astype(jnp.float32)
         )
-        stream_ref[span, :] = value.astype(jnp.bfloat16)
+        updated_ref[span, :] = value
         mean = jnp.sum(value, axis=1, keepdims=True) / width
         variance = jnp.sum(jnp.square(value - mean), axis=1, keepdims=True) / width
         lane = lax.broadcasted_iota(jnp.int32, (part, HD), 1)
         packed = jnp.where(lane == 0, mean, jnp.where(lane == 1, variance, 0.0))
         stat_out[p] = jnp.transpose(packed)[0:8]
-        updated.append(value)
 
     stat_in[tp] = stat_out[...]
     for i in range(1, tp_count):
@@ -434,19 +478,15 @@
             / tp_count
         )
         line = lax.broadcasted_iota(jnp.int32, (HD, part), 0)
-        packed = jnp.transpose(
+        stat_ref[pl.ds(p * part, part), :] = jnp.transpose(
             jnp.where(line == 0, row_mean, jnp.where(line == 1, lax.rsqrt(row_var + EPS), 0.0))
         )
-        normed = (updated[p] - packed[:, 0:1]) * packed[:, 1:2] * (
-            1.0 + scale_ref[...].astype(jnp.float32)
-        ) + shift_ref[...].astype(jnp.float32)
-        normed_ref[pl.ds(p * part, part), :] = normed.astype(jnp.bfloat16)
     for copy in copies:
         copy.wait_send()
     pltpu.make_async_copy(others, others, stat_sem.at[0]).wait()
 
 
-def project(attended, weight, residual, gate, shift, scale, tp_count):
+def project(attended, weight, residual, gate, tp_count):
     tokens, width = residual.shape
     part = tokens // 2
     vmem = pl.BlockSpec(memory_space=pltpu.VMEM)
@@ -455,8 +495,11 @@
     stat = pltpu.VMEM((2, 8, part), jnp.float32)
     return pl.pallas_call(
         project_kernel,
-        out_shape=(jax.ShapeDtypeStruct(residual.shape, jnp.bfloat16),) * 2,
-        in_specs=[vmem] * 6,
+        out_shape=(
+            jax.ShapeDtypeStruct(residual.shape, jnp.float32),
+            jax.ShapeDtypeStruct((tokens, HD), jnp.float32),
+        ),
+        in_specs=[vmem] * 4,
         out_specs=(vmem, vmem),
         scratch_shapes=[
             quad,
@@ -476,7 +519,7 @@
             pltpu.SemaphoreType.DMA((2,)),
         ],
         compiler_params=pltpu.CompilerParams(collective_id=1, has_side_effects=True),
-    )(attended, weight, residual, gate, shift, scale)
+    )(attended, weight, residual, gate)
 
 
 def shards(
@@ -564,15 +607,18 @@
         (resident_usable, arrived_usable),
         local_width,
     )
-    stream, normed = project(
+    updated, row_stats = project(
         attended,
         whole_weight.reshape(full_width, local_width),
         residual,
         gate,
-        shift,
-        scale,
         tp_count,
     )
+    stream = updated.astype(jnp.bfloat16)
+    normed = (
+        (updated - row_stats[:, :1]) * row_stats[:, 1:2] * (1.0 + scale.astype(jnp.float32))
+        + shift.astype(jnp.float32)
+    ).astype(jnp.bfloat16)
     return (stream, normed, cross_out)
 
 

time: 238 us -> 238 us (level)
  the two profiles are of different devices: /device:TPU:32 before, /device:TPU:16 now
where the time goes in v4:
time: 238 us; the launch traced here: 237 us
  Pallas kernels  216 us (91%)
  local copies, waits for them, and re-layouts  11.9 us (5%)
  other arithmetic  8.4 us (4%)
    pallas_call x1, Pallas kernels, exchange(): pl.pallas_call(functools.partial(exchange_kernel, layers), out_shape=(sha...  165 us
    pallas_call x1, Pallas kernels, project(): pl.pallas_call(project_kernel, out_shape=(jax.ShapeDtypeStruct(residual.s...  43.6 us
    pallas_call x1, Pallas kernels, per_head(): pl.pallas_call(kernel, grid=(width // HD,), out_shape=jax.ShapeDtypeStruc...  7.32 us

profile of v4, /device:TPU:16, one launch (start us, length us, event | category | flops | bytes accessed | tf_op | source)
XLA Modules:
  0.0 237.5 jit_solution(12715847018277761274)
XLA Ops:
  0.6 0.0 copy-start
  0.6 0.8 fusion.6
  1.5 0.1 reduce_window_sum.11
  1.6 0.8 fusion.8
  2.4 0.7 add_add_fusion
  3.1 0.7 select_reduce_fusion
  3.9 0.0 copy-start.1
  3.9 1.8 gather_fusion
  5.7 0.0 copy-done.1
  5.7 1.8 gather_fusion.1
  7.5 0.7 broadcast_in_dim.23.count_ref
  8.2 0.0 copy-done.2
  8.2 0.1 fusion
  8.4 0.1 fusion.3
  8.5 0.6 broadcast_in_dim.24.square_ref
  9.1 164.8 %shard_map.202 = (bf16[64,16,640]{2,1,0:T(8,128)(2,1)}, bf16[64,16,640]{2,1,0:T(8,128)(2,1)}, s32[64,1,128]{2,1,0:T(1,128)}, f32[8,2,1,256]{3,2,1,0:T(1,128)}, b...) custom-call(bf16[64,16,640]{2,1,0:T(8,128)(2,1)} %bitcast.26, bf16[64,16,640]{2,1,0:T(8,128)(2,1)} %bitcast.27, ...), custom_call_target="tpu_custom_call" | custom-call | tf_op jit(solution)/shard_map/pallas_call | solution.py:312
  173.9 0.0 copy-start.10
  173.9 0.8 reduce_sum.62
  174.7 1.1 fusion.2
  175.8 1.3 slice_reduce_fusion.2
  177.0 0.1 fusion.7
  177.1 0.1 broadcast_in_dim.25
  177.2 0.7 reshape.151.ua_ref
  178.0 1.5 gather_fusion.2
  179.5 1.4 gather_fusion.3
  181.5 0.6 compare_convert_fusion.ur_ref
  182.1 7.3 %shard_map.203.attended_ref = bf16[256,640]{1,0:T(8,128)(2,1)} custom-call(bf16[256,640]{1,0:T(8,128)(2,1)} %get-tuple-element.27.q_ref, bf16[384,640]{1,0:T(8,128)(2,1)} %bitcast.28, bf16[384,640]{1,0:T(8,128)(2,1)} %bitcast.29, bf16[1024,640]{1,0:T(8,128)(2,1)} %bitcast.30, bf16[1024,640]{1,0:T(8,128)(2,1)} %bitcast.31, ...), custom_call_target="tpu_custom_call" | custom-call | flops 1090519040 | bytes 4915200 | tf_op jit(solution)/shard_map/pallas_call | solution.py:61
  189.5 43.6 %shard_map.204 = (f32[256,640]{1,0:T(8,128)}, f32[256,128]{1,0:T(8,128)}) custom-call(bf16[256,640]{1,0:T(8,128)(2,1)} %shard_map.203.attended_ref, bf16[5120,640]{1,0:T(8,128)(2,1)} %bitcast.25, bf16[256,640]{1,0:T(8,128)(2,1)} %residual_ref.1, bf16[1,640]{1,0:T(2,128)(2,1)} %gate_ref.1), custom_call_target="tpu_custom_call" | custom-call | tf_op jit(solution)/shard_map/pallas_call | solution.py:496
  233.1 1.2 slice_reduce_fusion.1
  234.4 2.4 %add_convert_fusion = (bf16[256,640]{1,0:T(8,128)(2,1)}, bf16[256,640]{1,0:T(8,128)(2,1)}) fusion(f32[256,640]{1,0:T(8,128)} %get-tuple-element.16, f32[640]{0:T(1024)S(1)} %get-tuple-element.29, f32[640]{0:T(1024)S(1)} %get-tuple-element.30, f32[256]{0:T(256)S(1)} %get-tuple-element.20, f32[256]{0:T(256)S(1)} %get-tuple-element.19), kind=kLoop, calls=%fused_computation.14 | loop fusion | flops 983040 | bytes 1317888 | tf_op jit(solution)/shard_map/convert_element_type | solution.py:621
  236.8 0.0 copy-done.4
  236.8 0.7 copy.24
  (23 shorter events, 0.1 us)
Async XLA Ops:
  0.6 3.2 %copy-start = (bf16[112,8,640]{2,1,0:T(8,128)(2,1)S(1)}, bf16[112,8,640]{2,1,0:T(8,128)(2,1)}, u32[]{:S(2)}) copy-start(bf16[112,8,640]{2,1,0:T(8,128)(2,1)} %param.24) | copy-start | bytes 3440644
  3.9 1.8 copy-start.1
  5.7 2.5 %copy-start.2 = (bf16[256,640]{1,0:T(8,128)(2,1)S(1)}, bf16[256,640]{1,0:T(8,128)(2,1)}, u32[]{:S(2)}) copy-start(bf16[256,640]{1,0:T(8,128)(2,1)} %param.19) | copy-start | bytes 983044
  5.7 2.7 %copy-start.3 = (bf16[256,640]{1,0:T(8,128)(2,1)S(1)}, bf16[256,640]{1,0:T(8,128)(2,1)}, u32[]{:S(2)}) copy-start(bf16[256,640]{1,0:T(8,128)(2,1)} %param.20) | copy-start | bytes 983044
  9.1 165.6 %copy-start.6 = (f32[640]{0:T(1024)S(1)}, f32[640]{0:T(1024)}, u32[]{:S(2)}) copy-start(f32[640]{0:T(1024)} %param.22) | copy-start | bytes 7684
  9.1 165.6 %copy-start.7 = (f32[640]{0:T(1024)S(1)}, f32[640]{0:T(1024)}, u32[]{:S(2)}) copy-start(f32[640]{0:T(1024)} %param.23) | copy-start | bytes 7684
  173.9 1.9 copy-start.5
  173.9 4.1 %copy-start.10 = (s32[1,48]{1,0:T(1,128)S(1)}, s32[1,48]{1,0:T(1,128)}, u32[]{:S(2)}) copy-start(s32[1,48]{1,0:T(1,128)} %param.26) | copy-start | bytes 580
  189.4 44.9 %copy-start.8 = (bf16[1,640]{1,0:T(2,128)(2,1)S(1)}, bf16[1,640]{1,0:T(2,128)(2,1)}, u32[]{:S(2)}) copy-start(bf16[1,640]{1,0:T(2,128)(2,1)} %param.36) | copy-start | bytes 3844
  189.4 44.9 %copy-start.9 = (bf16[1,640]{1,0:T(2,128)(2,1)S(1)}, bf16[1,640]{1,0:T(2,128)(2,1)}, u32[]{:S(2)}) copy-start(bf16[1,640]{1,0:T(2,128)(2,1)} %param.37) | copy-start | bytes 3844
  233.1 3.7 %copy-start.4 = (bf16[256,640]{1,0:T(8,128)(2,1)S(1)}, bf16[256,640]{1,0:T(8,128)(2,1)}, u32[]{:S(2)}) copy-start(bf16[256,640]{1,0:T(8,128)(2,1)} %get-tuple-element.36) | copy-start | bytes 983044

commit v5 on v3

--- a/solution.py
+++ b/solution.py
@@ -192,7 +192,8 @@
     send_weight(weight_ref, req, beside, core_recv)
     right_steps = layers // 2
     left_steps = layers - 1 - right_steps
-    batch(0)
+    for h, c in ((0, 1), (1, 0), (1, 1)):
+        send_pages(place((half + h) % 2, layer, (core + c) % 2))
 
     def step(s, from_left, from_right):
         if from_left is not None:
@@ -211,7 +212,7 @@
                 send_weight(weight_out.at[origin], origin, left, left_recv.at[s + 1])
             send_weight(weight_out.at[origin], origin, across, row_recv.at[z])
             send_weight(weight_out.at[origin], origin, beside, core_recv)
-        batch(s + 1)
+        batch(layers - 2 - s)
 
     @pl.loop(0, left_steps - 1)
     def _(s):
@@ -220,12 +221,10 @@
     for s in range(left_steps - 1, right_steps):
         step(s, s < right_steps - 1, s < left_steps - 1 if s < left_steps else None)
 
-    @pl.loop(right_steps + 1, layers - 1)
+    @pl.loop(0, layers - 1 - right_steps)
     def _(k):
         batch(k)
 
-    for h, c in ((0, 1), (1, 0), (1, 1)):
-        send_pages(place((half + h) % 2, layer, (core + c) % 2))
 
     @pl.loop(0, layers)
     def _(s):

time: 238 us -> 234 us (0.983)
  the two profiles are of different devices: /device:TPU:32 before, /device:TPU:56 now
where the time goes in v5:
time: 234 us
  Pallas kernels  212 us (91%)
  local copies, waits for them, and re-layouts  14.2 us (6%)
  other arithmetic  5.98 us (3%)
    pallas_call x1, Pallas kernels, exchange(): pl.pallas_call(functools.partial(exchange_kernel, layers), out_shape=(sha...  159 us
    pallas_call x1, Pallas kernels, project(): pl.pallas_call(project_kernel, out_shape=(jax.ShapeDtypeStruct(residual.s...  45.7 us
    pallas_call x1, Pallas kernels, per_head(): pl.pallas_call(kernel, grid=(width // HD,), out_shape=jax.ShapeDtypeStruc...  7.32 us

profile of v5, /device:TPU:56, one launch (start us, length us, event | category | flops | bytes accessed | tf_op | source)
XLA Modules:
  0.0 233.6 jit_solution(6695034799311887857)
XLA Ops:
  0.6 0.0 copy-start
  0.6 0.8 fusion.6
  1.5 0.1 reduce_window_sum.11
  1.6 0.8 fusion.8
  2.4 0.7 add_add_fusion
  3.1 0.7 select_reduce_fusion
  3.9 0.0 copy-start.1
  3.9 1.8 gather_fusion
  5.7 0.0 copy-done.1
  5.7 1.8 gather_fusion.1
  7.5 0.7 broadcast_in_dim.23.count_ref
  8.2 0.1 fusion
  8.4 0.0 copy-done.3
  8.4 0.1 fusion.3
  8.5 0.6 broadcast_in_dim.24.square_ref
  9.1 159.0 %shard_map.202 = (bf16[64,16,640]{2,1,0:T(8,128)(2,1)}, bf16[64,16,640]{2,1,0:T(8,128)(2,1)}, s32[64,1,128]{2,1,0:T(1,128)}, f32[8,2,1,256]{3,2,1,0:T(1,128)}, b...) custom-call(bf16[64,16,640]{2,1,0:T(8,128)(2,1)} %bitcast.26, bf16[64,16,640]{2,1,0:T(8,128)(2,1)} %bitcast.27, ...), custom_call_target="tpu_custom_call" | custom-call | tf_op jit(solution)/shard_map/pallas_call | solution.py:266
  168.1 0.0 copy-start.8
  168.1 0.8 reduce_sum.62
  168.9 1.1 fusion.2
  170.0 0.0 copy-done.5
  170.0 1.3 slice_reduce_fusion
  171.2 0.1 fusion.7
  171.3 0.1 broadcast_in_dim.25
  171.4 0.7 reshape.151.ua_ref
  172.2 1.5 gather_fusion.2
  173.7 1.4 gather_fusion.3
  175.7 0.6 compare_convert_fusion.ur_ref
  176.3 7.3 %shard_map.203.attended_ref = bf16[256,640]{1,0:T(8,128)(2,1)} custom-call(bf16[256,640]{1,0:T(8,128)(2,1)} %get-tuple-element.23.q_ref, bf16[384,640]{1,0:T(8,128)(2,1)} %bitcast.28, bf16[384,640]{1,0:T(8,128)(2,1)} %bitcast.29, bf16[1024,640]{1,0:T(8,128)(2,1)} %bitcast.30, bf16[1024,640]{1,0:T(8,128)(2,1)} %bitcast.31, ...), custom_call_target="tpu_custom_call" | custom-call | flops 1090519040 | bytes 4915200 | tf_op jit(solution)/shard_map/pallas_call | solution.py:61
  183.6 45.7 %shard_map.204 = (bf16[256,640]{1,0:T(8,128)(2,1)}, bf16[256,640]{1,0:T(8,128)(2,1)}) custom-call(bf16[256,640]{1,0:T(8,128)(2,1)} %shard_map.203.attended_ref, bf16[5120,640]{1,0:T(8,128)(2,1)} %bitcast.25, bf16[256,640]{1,0:T(8,128)(2,1)} %residual_ref.1, bf16[1,640]{1,0:T(2,128)(2,1)} %gate_ref.1, bf16[1,640]{1,0:T(2,128)(2,1)} %shift_ref.1, ...), custom_call_target="tpu_custom_call" | custom-call | tf_op jit(solution)/shard_map/pallas_call | solution.py:455
  229.4 1.8 copy.26
  231.1 1.7 copy.27
  232.9 0.7 copy.28
  (18 shorter events, 0.1 us)
Async XLA Ops:
  0.6 3.2 %copy-start = (bf16[112,8,640]{2,1,0:T(8,128)(2,1)S(1)}, bf16[112,8,640]{2,1,0:T(8,128)(2,1)}, u32[]{:S(2)}) copy-start(bf16[112,8,640]{2,1,0:T(8,128)(2,1)} %param.24) | copy-start | bytes 3440644
  3.9 1.8 copy-start.1
  5.7 2.6 %copy-start.2 = (bf16[256,640]{1,0:T(8,128)(2,1)S(1)}, bf16[256,640]{1,0:T(8,128)(2,1)}, u32[]{:S(2)}) copy-start(bf16[256,640]{1,0:T(8,128)(2,1)} %param.19) | copy-start | bytes 983044
  5.7 2.7 %copy-start.3 = (bf16[256,640]{1,0:T(8,128)(2,1)S(1)}, bf16[256,640]{1,0:T(8,128)(2,1)}, u32[]{:S(2)}) copy-start(bf16[256,640]{1,0:T(8,128)(2,1)} %param.20) | copy-start | bytes 983044
  9.1 159.8 %copy-start.6 = (f32[640]{0:T(1024)S(1)}, f32[640]{0:T(1024)}, u32[]{:S(2)}) copy-start(f32[640]{0:T(1024)} %param.22) | copy-start | bytes 7684
  9.1 159.8 %copy-start.7 = (f32[640]{0:T(1024)S(1)}, f32[640]{0:T(1024)}, u32[]{:S(2)}) copy-start(f32[640]{0:T(1024)} %param.23) | copy-start | bytes 7684
  168.1 1.9 copy-start.5
  168.1 4.1 %copy-start.8 = (s32[1,48]{1,0:T(1,128)S(1)}, s32[1,48]{1,0:T(1,128)}, u32[]{:S(2)}) copy-start(s32[1,48]{1,0:T(1,128)} %param.26) | copy-start | bytes 580
  229.3 3.5 %copy-start.4 = (bf16[256,640]{1,0:T(8,128)(2,1)S(1)}, bf16[256,640]{1,0:T(8,128)(2,1)}, u32[]{:S(2)}) copy-start(bf16[256,640]{1,0:T(8,128)(2,1)} %get-tuple-element.30) | copy-start | bytes 983044
